TPU v7x, 128 devices: a whole 4x4x4 slice. The times are simulated.
128 devices in a mesh: req: 8 (over x, core), exp: 16 (over y, z).
Axes of the slice: x: 4, y: 4, z: 4, core: 2. Of those that a mesh axis runs over, the one named last changes fastest.
Arguments:
- tokens: bfloat16 [16384, 2048], P(('req', 'exp')), may hold values from -6 to 6
- norm_gains: float32 [2, 2048], replicated, may hold values from 0.25 to 1.75
- w_query: bfloat16 [2048, 4, 2048], P(None, None, 'exp'), may hold values from -0.125 to 0.125
- w_keyval: bfloat16 [2048, 2, 2048], P(None, None, 'exp'), may hold values from -0.125 to 0.125
- w_out: bfloat16 [4, 2048, 2048], P(None, 'exp'), may hold values from -0.125 to 0.125
- page_pool: bfloat16 [32, 128, 16, 256], P('req', None, 'exp'), may hold values from -3000 to 3000
- page_dest: int32 [32], replicated, may hold values from 0 to 31, as said below
- prompt_lens: int32 [8, 4], P('req'), may hold values from 1 to 1024, 2048 in all within a row
- att_ids: int32 [16384, 2], P('req'), may hold values from 0 to 3, all different within a row
- att_gates: float32 [16384, 2], P('req'), may hold values from 0.1 to 1
- w_in: bfloat16 [2048, 2, 22528], P(None, None, 'exp'), may hold values from -0.125 to 0.125
- w_down: bfloat16 [22528, 2048], P('exp'), may hold values from -0.109375 to 0.109375
- moe_ids: int32 [16384, 2], P(('req', 'exp')), may hold values from 0 to 7, all different within a row; in each aligned block of 128 rows (0 to 127, 128 to 255, ...) at most 40 rows name the same one
- moe_gates: float32 [16384, 2], P(('req', 'exp')), may hold values from 0.1 to 1
- adapters: bfloat16 [64, 2, 16, 2048], P('exp'), may hold values from -0.25 to 0.25
- req_adapter: int32 [32], replicated, may hold values from 0 to 63, as said below
Outputs:
- layer_out: bfloat16 [16384, 2048], P(('req', 'exp'))
Inputs may be any that keep to these rules, and one draw needn't show every extreme that they name: `page_dest`: pool slot g * 4 + p holds the pages of request ((g + s_p) mod the number of groups) * 4 + p, where the 4 shifts s_p are distinct: a group's slots go to 4 different groups, and each group receives one request a slot. `prompt_lens`: the 4 lengths of a group sum to 2048. `att_ids`: the two ids of a token differ. `moe_ids`: the two ids of a token differ; among the 128 tokens of one device no expert is named by more than 40, a bound that some block reaches. `req_adapter`: exactly 16 distinct adapters are named, adapters 0 and 63 among them.
All inputs are finite; a program needn't handle non-finite values.
Results may differ from a plain program's by a relative error of at most 0.015.
Values may be sent and summed in bfloat16 or wider, within the bound.
A program may use at most 192 MiB of HBM per device.

v0:
```python
import math

import jax
import jax.numpy as jnp
from jax import lax
from jax.sharding import PartitionSpec as P

HD = 128
AEXP = 4
EXPERTS = 8
CACHE = 128
CAP = 40


norm_eps = 1e-05


def rms_scale(values, gain):
    values = values.astype(jnp.float32)
    factor = lax.rsqrt(jnp.mean(values * values, axis=-1, keepdims=True) + norm_eps)
    return (values * factor * gain).astype(jnp.bfloat16)


def rotate(vectors, places):
    half_width = vectors.shape[-1] // 2
    steps_idx = jnp.arange(half_width, dtype=jnp.float32)
    inverse = jnp.power(10000.0, steps_idx * (-2.0 / vectors.shape[-1]))
    angles = places.astype(jnp.float32)[:, None] * inverse[None, :]
    angles = angles.reshape((places.shape[0],) + (1,) * (vectors.ndim - 2) + (half_width,))
    cosine = jnp.cos(angles)
    sine_part = jnp.sin(angles)
    former = vectors[..., :half_width]
    latter = vectors[..., half_width:]
    return jnp.concatenate(
        [former * cosine - latter * sine_part, former * sine_part + latter * cosine], axis=-1
    )


def group_positions(lengths, total, cached):
    finish = jnp.cumsum(lengths)
    beginning = finish - lengths
    indices = jnp.arange(total, dtype=jnp.int32)
    segment = jnp.sum((indices[:, None] >= finish[None, :]).astype(jnp.int32), axis=1)
    member = segment[:, None] == jnp.arange(lengths.shape[0], dtype=jnp.int32)[None, :]
    offset = jnp.sum(jnp.where(member, beginning[None, :], 0), axis=1)
    return (segment, cached + indices - offset)


def attend_block(queries, key_rows, val_rows, visible, scale_factor):
    scores = (
        jnp.einsum("qhd,khd->hqk", queries, key_rows, preferred_element_type=jnp.float32)
        * scale_factor
    )
    scores = jnp.where(visible[None, :, :], scores, -1e30)
    highest = jnp.max(scores, axis=-1, keepdims=True)
    raised = jnp.exp(scores - highest)
    weights = (raised / jnp.sum(raised, axis=-1, keepdims=True)).astype(jnp.bfloat16)
    return jnp.einsum("hqk,khd->qhd", weights, val_rows, preferred_element_type=jnp.float32).astype(
        jnp.bfloat16
    )


def on_device(
    tokens,
    norm_gains,
    w_query,
    w_keyval,
    w_out,
    page_pool,
    page_dest,
    prompt_lens,
    att_ids,
    att_gates,
    w_in,
    w_down,
    moe_ids,
    moe_gates,
    adapters,
    req_adapter,
):
    groups = lax.axis_size("req")
    columns = lax.axis_size("exp")
    group_index = lax.axis_index("req")
    column_index = lax.axis_index("exp")
    tok_rows = tokens.shape[0]
    width = tokens.shape[1]
    group_rows = tok_rows * columns
    local_heads = w_query.shape[2] // HD
    slot_count = page_pool.shape[0]
    group_numbers = jnp.arange(groups, dtype=jnp.int32)
    own_target = (
        lax.dynamic_slice_in_dim(page_dest, group_index * slot_count, slot_count) // slot_count
    )
    outgoing_map = (own_target[None, :] == group_numbers[:, None]).astype(jnp.bfloat16)
    outgoing = jnp.dot(
        outgoing_map, page_pool.reshape(slot_count, -1), preferred_element_type=jnp.float32
    )
    outgoing = outgoing.astype(jnp.bfloat16).reshape((groups,) + page_pool.shape[1:])
    incoming = lax.all_to_all(outgoing, "req", split_axis=0, concat_axis=0, tiled=True)
    pool_slots = jnp.arange(page_dest.shape[0], dtype=jnp.int32)
    wanted = group_index * slot_count + jnp.arange(slot_count, dtype=jnp.int32)
    sender = (
        jnp.sum(jnp.where(page_dest[None, :] == wanted[:, None], pool_slots[None, :], 0), axis=1)
        // slot_count
    )
    incoming_map = (sender[:, None] == group_numbers[None, :]).astype(jnp.bfloat16)
    cached = jnp.dot(incoming_map, incoming.reshape(groups, -1), preferred_element_type=jnp.float32)
    cached = cached.astype(jnp.bfloat16).reshape(page_pool.shape)
    segment, places = group_positions(prompt_lens.reshape(-1), group_rows, CACHE)
    normed = rms_scale(tokens, norm_gains[0])
    gathered, factor_table = (
        lax.all_gather(normed, "exp", axis=0, tiled=True),
        lax.all_gather(adapters, "exp", axis=0, tiled=True),
    )
    queries = jnp.dot(gathered, w_query.reshape(width, -1), preferred_element_type=jnp.float32)
    queries = rotate(queries.reshape(group_rows, AEXP, local_heads, HD), places).astype(
        jnp.bfloat16
    )
    chosen_rows = (jnp.arange(group_rows, dtype=jnp.int32)[:, None] * AEXP + att_ids).reshape(-1)
    chosen = jnp.take(queries.reshape(group_rows * AEXP, local_heads * HD), chosen_rows, axis=0)
    keyval = jnp.dot(gathered, w_keyval.reshape(width, -1), preferred_element_type=jnp.float32)
    keyval = keyval.reshape(group_rows, 2, local_heads, HD)
    new_keys = rotate(keyval[:, 0], places).astype(jnp.bfloat16)
    new_values = keyval[:, 1].astype(jnp.bfloat16)
    key_rows = jnp.concatenate([cached[..., :HD].reshape(-1, local_heads, HD), new_keys], axis=0)
    val_rows = jnp.concatenate([cached[..., HD:].reshape(-1, local_heads, HD), new_values], axis=0)
    key_segment = jnp.concatenate(
        [jnp.repeat(jnp.arange(slot_count, dtype=jnp.int32), CACHE), segment]
    )
    key_index = jnp.concatenate(
        [jnp.full((slot_count * CACHE,), -1, jnp.int32), jnp.arange(group_rows, dtype=jnp.int32)]
    )
    query_total = 2 * group_rows
    block_rows = 1024
    block_count = query_total // block_rows
    query_segment = jnp.repeat(segment, 2).reshape(block_count, block_rows)
    query_index = jnp.repeat(jnp.arange(group_rows, dtype=jnp.int32), 2).reshape(
        block_count, block_rows
    )
    scale_factor = 1.0 / math.sqrt(HD)

    def block_step(items):
        block_queries, block_segment, block_index = items
        visible = (block_segment[:, None] == key_segment[None, :]) & (
            key_index[None, :] <= block_index[:, None]
        )
        return attend_block(block_queries, key_rows, val_rows, visible, scale_factor)

    heads_out = lax.map(
        block_step,
        (chosen.reshape(block_count, block_rows, local_heads, HD), query_segment, query_index),
    )
    heads_out = heads_out.reshape(group_rows, 2, local_heads * HD)
    slot_weights = jnp.where(
        att_ids[:, :, None] == jnp.arange(AEXP, dtype=jnp.int32)[None, None, :],
        att_gates[:, :, None],
        0.0,
    )
    mixed = jnp.einsum(
        "tje,tjx->tex", slot_weights, heads_out.astype(jnp.float32), precision=lax.Precision.HIGHEST
    ).astype(jnp.bfloat16)
    flat_mixed = mixed.reshape(group_rows, -1)
    flat_out = w_out.reshape(-1, width)
    attended = lax.psum_scatter(
        jnp.dot(flat_mixed, flat_out, preferred_element_type=jnp.float32).astype(jnp.bfloat16),
        "exp",
        scatter_dimension=0,
        tiled=True,
    ).astype(jnp.float32)
    hidden_state = (tokens.astype(jnp.float32) + attended).astype(jnp.bfloat16)
    hnorm = rms_scale(hidden_state, norm_gains[1])
    expert_flat = moe_ids.reshape(-1)
    expert_hits = (expert_flat[:, None] == jnp.arange(EXPERTS, dtype=jnp.int32)[None, :]).astype(
        jnp.int32
    )
    earlier = jnp.cumsum(expert_hits, axis=0) - expert_hits
    route_slot = jnp.sum(earlier * expert_hits, axis=1) + expert_flat * CAP
    table_size = EXPERTS * CAP
    placing = (jnp.arange(table_size, dtype=jnp.int32)[:, None] == route_slot[None, :]).reshape(
        table_size, tok_rows, 2
    )
    placing = jnp.any(placing, axis=2).astype(jnp.bfloat16)
    packed = jnp.dot(placing, hnorm, preferred_element_type=jnp.float32).astype(jnp.bfloat16)
    packed = packed.reshape(EXPERTS, CAP, width)
    copies = columns // EXPERTS
    spread_rows = jnp.repeat(packed, copies, axis=0)
    arrived = lax.all_to_all(spread_rows, "exp", split_axis=0, concat_axis=0, tiled=True)
    flat_rows = arrived.reshape(-1, width)
    gate_up = jnp.einsum("nd,dkf->nkf", flat_rows, w_in, preferred_element_type=jnp.float32)
    inner_act = (jax.nn.silu(gate_up[:, 0]) * gate_up[:, 1]).astype(jnp.bfloat16)
    partial_out = jnp.dot(inner_act, w_down, preferred_element_type=jnp.float32).reshape(
        columns, CAP, width
    )
    returned = lax.all_to_all(
        partial_out.astype(jnp.bfloat16), "exp", split_axis=0, concat_axis=0, tiled=True
    ).astype(partial_out.dtype)
    summed = jnp.sum(returned.reshape(EXPERTS, copies, CAP, width), axis=1).reshape(
        table_size, width
    )
    routed_rows = jnp.take(summed, route_slot, axis=0).reshape(tok_rows, 2, width)
    expert_out = jnp.sum(routed_rows * moe_gates[:, :, None], axis=1)
    own_segment = lax.dynamic_slice_in_dim(segment, column_index * tok_rows, tok_rows)
    wanted_ids = lax.dynamic_slice_in_dim(req_adapter, group_index * slot_count, slot_count)
    group_factors = jnp.take(factor_table, wanted_ids, axis=0)
    lowrank = jnp.einsum(
        "td,qrd->tqr", hnorm, group_factors[:, 0], preferred_element_type=jnp.float32
    )
    member = own_segment[:, None] == jnp.arange(slot_count, dtype=jnp.int32)[None, :]
    lowrank = jnp.where(member[:, :, None], lowrank, 0.0).astype(jnp.bfloat16)
    delta = jnp.einsum(
        "tqr,qrd->td", lowrank, group_factors[:, 1], preferred_element_type=jnp.float32
    )
    return (hidden_state.astype(jnp.float32) + expert_out + delta).astype(jnp.bfloat16)


def solution(mesh):
    in_specs = (
        P(("req", "exp"), None),
        P(),
        P(None, None, "exp"),
        P(None, None, "exp"),
        P(None, "exp", None),
        P("req", None, "exp", None),
        P(),
        P("req", None),
        P("req", None),
        P("req", None),
        P(None, None, "exp"),
        P("exp", None),
        P(("req", "exp"), None),
        P(("req", "exp"), None),
        P("exp", None, None, None),
        P(),
    )
    out_specs = P(("req", "exp"), None)
    return jax.shard_map(
        on_device, mesh=mesh, in_specs=in_specs, out_specs=out_specs, check_vma=False
    )
```

profile of v0, /device:TPU:14, one launch (start us, length us, event | category | flops | bytes accessed | tf_op | source)
XLA Modules:
  0.0 428.7 jit_solution(572273095030612041)
XLA Ops:
  13.8 4.9 %all-to-all-start = ((bf16[8,128,1,256]{3,1,2,0:T(8,128)(2,1)}), bf16[8,128,1,256]{3,1,2,0:T(8,128)(2,1)}, u32[]{:S(2)}, u32[]{:S(2)}) async-start(bf16[8,128,1,256]{3,1,2,0:T(8,128)(2,1)} %copy.128), calls=%async_computation | async-start | bytes 1048576 | tf_op jit(solution)/shard_map/all_to_all | solution.py:99
  21.9 3.4 copy.159
  25.3 4.3 copy.123
  42.7 41.9 %all-gather.3.cloned.1.call-done = bf16[2048,2048]{1,0:T(8,128)(2,1)} async-done(((bf16[128,2048]{1,0:T(8,128)(2,1)}), bf16[2048,2048]{1,0:T(8,128)(2,1)}) %all-gather.3.cloned.1.call-update) | async-done | bytes 8388624 | tf_op jit(solution)/shard_map/all_gather | solution.py:112
  84.7 5.9 %fusion.24 = f32[2048,2,1,128]{0,3,1,2:T(8,128)S(1)} fusion(bf16[2,128,2048]{2,1,0:T(8,128)(2,1)S(1)} %bitcast.178, bf16[2048,2048]{1,0:T(8,128)(2,1)} %all-gather.3.cloned.1.call-done), kind=kOutput, calls=%fused_computation.34 | convolution fusion | flops 2147483648 | bytes 11534336 | tf_op jit(solution)/shard_map/dot_general | solution.py:121
  92.5 4.5 %fusion.18 = f32[2048,4,1,128]{0,3,1,2:T(8,128)S(1)} fusion(bf16[4,128,2048]{2,1,0:T(8,128)(2,1)S(1)} %bitcast.173, bf16[2048,2048]{1,0:T(8,128)(2,1)S(1)} %copy-done.22), kind=kOutput, calls=%fused_computation.32 | convolution fusion | flops 4294967296 | bytes 14680064 | tf_op jit(solution)/shard_map/dot_general | solution.py:115
  98.8 4.1 copy.124
  105.3 4.3 %fusion.49 = (bf16[2048,1,64]{0,2,1:T(8,128)(2,1)S(1)}, bf16[2048,1,64]{0,2,1:T(8,128)(2,1)S(1)}) fusion(f32[2048,1,128]{0,2,1:T(8,128)} %slice_bitcast_fusion, f32[64]{0:T(128)} %copy-done.19, f32[2048]{0:T(1024)} %copy-done.11), kind=kLoop, calls=%fused_computation.81 | loop fusion | flops 1179648 | bytes 1581312 | tf_op jit(solution)/shard_map/convert.2
  111.9 4.7 %pad_maximum_fusion = bf16[8192,128]{1,0:T(8,128)(2,1)} fusion(bf16[8192,64]{1,0:T(8,128)(2,1)} %bitcast.164, bf16[8192,64]{1,0:T(8,128)(2,1)} %bitcast.163), kind=kLoop, calls=%fused_computation.40 | loop fusion | flops 4194304 | bytes 4194304 | tf_op jit(solution)/shard_map/concatenate | solution.py:34
  116.7 12.9 %gather_fusion = bf16[4096,128]{1,0:T(8,128)(2,1)S(1)} fusion(bf16[8192,128]{1,0:T(8,128)(2,1)} %pad_maximum_fusion, s32[4096]{0:T(1024)S(1)} %copy-done.14), kind=kCustom, calls=%fused_computation | custom fusion | bytes 2113536 | tf_op jit(solution)/shard_map/jit(_take)/gather | solution.py:120
  131.7 36.9 %while.11 = (s32[]{:T(128)}, bf16[4,1024,1,128]{3,1,2,0:T(8,128)(2,1)}, s32[4,1024]{1,0:T(4,128)}, s32[2560]{0:T(1024)S(1)}, s32[4,1024]{1,0:T(4,128)S(1)}, /*in...) while((s32[]{:T(128)}, ...), condition=%wide.region_8.9_spmd, body=%wide.region_5.8_spmd.sunk | while | flops 1371142144 | bytes 35980420 | solution.py:149
  132.6 4.0 fusion.96
  138.2 2.9 fusion.98
  141.8 4.0 fusion.96
  147.4 2.9 fusion.98
  151.0 4.0 fusion.96
  156.6 2.9 fusion.98
  160.2 4.0 fusion.96
  168.7 14.3 %fusion.31 = bf16[2048,4,128]{2,1,0:T(4,128)(2,1)S(1)} fusion(bf16[2048,2,128]{2,1,0:T(2,128)(2,1)} %bitcast.33, f32[2048,2]{1,0:T(8,128)} %copy.120, s32[2048,2]{1,0:T(8,128)S(1)} %copy-done.7), kind=kOutput, calls=%fused_computation.46 | convolution fusion | flops 26247168 | bytes 3178496 | tf_op jit(solution)/shard_map/tje,tjx->tex/dot_general | solution.py:159
  183.0 6.5 %bitcast_convert_fusion = bf16[2048,2048]{1,0:T(8,128)(2,1)} fusion(bf16[4,128,2048]{2,1,0:T(8,128)(2,1)S(1)} %copy-done, bf16[2048,4,128]{2,1,0:T(4,128)(2,1)S(1)} %fusion.31), kind=kOutput, calls=%fused_computation.20 | convolution fusion | flops 4299161600 | bytes 12582912 | tf_op jit(solution)/shard_map/dot_general | solution.py:165
  191.9 83.3 %reduce-scatter.2.cloned.1.call-done = bf16[128,2048]{1,0:T(8,128)(2,1)} async-done(((bf16[2048,2048]{1,0:T(8,128)(2,1)}), bf16[128,2048]{1,0:T(8,128)(2,1)}) %reduce-scatter.2.cloned.1.call-update) | async-done | bytes 524304 | tf_op jit(solution)/shard_map/reduce_scatter | solution.py:164
  278.5 45.0 %all_to_all.15 = bf16[16,40,2048]{2,1,0:T(8,128)(2,1)S(1)} all-to-all(bf16[16,40,2048]{2,1,0:T(8,128)(2,1)S(1)} %bitcast.162), channel_id=1, replica_groups=mesh['req'=8,'exp'=16] {'exp'}, dimensions={0} | all-to-all | bytes 5242880 | tf_op jit(solution)/shard_map/all_to_all | solution.py:187
  323.5 11.9 %fusion.10 = f32[640,2,1408]{2,0,1:T(8,128)S(1)} fusion(bf16[640,2048,1]{1,0,2:T(8,128)(2,1)S(1)} %bitcast.171, bf16[2048,2,1408]{2,1,0:T(2,128)(2,1)} %param.28), kind=kOutput, calls=%fused_computation.21 | convolution fusion | flops 7381975040 | bytes 21364736 | tf_op jit(solution)/shard_map/nd,dkf->nkf/dot_general | solution.py:189
  335.9 6.1 %fusion.21 = bf16[16,40,2048]{2,1,0:T(8,128)(2,1)} fusion(bf16[1408,2048]{1,0:T(8,128)(2,1)S(1)} %bitcast.195, f32[16,40,1408]{2,1,0:T(8,128)S(1)} %bitcast.170, f32[16,40,1408]{2,1,0:T(8,128)S(1)} %bitcast.169), kind=kOutput, calls=%fused_computation.33 | convolution fusion | flops 3697704960 | bytes 15597568 | tf_op jit(solution)/shard_map/dot_general | solution.py:191
  342.0 6.5 %all-to-all-start.2 = ((bf16[16,40,2048]{2,1,0:T(8,128)(2,1)}), bf16[16,40,2048]{2,1,0:T(8,128)(2,1)}, u32[]{:S(2)}, u32[]{:S(2)}) async-start(bf16[16,40,2048]{2,1,0:T(8,128)(2,1)} %fusion.21), calls=%async_computation.3 | async-start | bytes 5242880 | tf_op jit(solution)/shard_map/all_to_all | solution.py:194
  349.9 44.4 %all-gather.5.cloned.1.call-done = bf16[64,2,16,2048]{3,2,1,0:T(8,128)(2,1)} async-done(((bf16[4,2,16,2048]{3,2,1,0:T(8,128)(2,1)}), bf16[64,2,16,2048]{3,2,1,0:T(8,128)(2,1)}) %all-gather.5.cloned.1.call-update) | async-done | bytes 8388624 | tf_op jit(solution)/shard_map/all_gather | solution.py:113
  394.3 4.0 gather_fusion.2
  399.2 4.1 convert_reduce_fusion
  403.3 5.3 %gather_fusion.1 = f32[256,2048]{1,0:T(8,128)} fusion(f32[320,2048]{1,0:T(8,128)} %bitcast.161, s32[1024]{0:T(1024)S(1)} %pad_clamp_fusion.1), kind=kCustom, calls=%fused_computation.1 | custom fusion | bytes 4195328 | tf_op jit(solution)/shard_map/jit(_take)/gather | solution.py:200
  408.7 3.5 gather.19
  412.2 6.6 %multiply_reduce_fusion = f32[128,2048]{1,0:T(8,128)} fusion(f32[128,2,2048]{2,1,0:T(2,128)} %gather.19, pred[128,2]{1,0:T(8,128)(4,1)S(1)} %copy.139, f32[128,2]{1,0:T(8,128)S(1)} %copy.142), kind=kLoop, calls=%fused_computation.42 | loop fusion | flops 1310720 | bytes 3147008 | tf_op jit(solution)/shard_map/reduce_sum | solution.py:201
  418.8 3.1 fusion.28
  (164 shorter events, 54.4 us)
Async XLA Ops:
  6.5 176.5 %copy-start = (bf16[4,128,2048]{2,1,0:T(8,128)(2,1)S(1)}, bf16[4,128,2048]{2,1,0:T(8,128)(2,1)}, u32[]{:S(2)}) copy-start(bf16[4,128,2048]{2,1,0:T(8,128)(2,1)} %param.22) | copy-start | bytes 6291460
  6.5 6.0 %copy-start.23 = (s32[32]{0:T(128)S(1)}, s32[32]{0:T(128)}, u32[]{:S(2)}) copy-start(s32[32]{0:T(128)} %param.24) | copy-start | bytes 388
  6.5 78.1 %all-gather.3.cloned.1.call-start = ((), (), s32[]{:S(2)}) async-start(), calls=%async_computation.4 | async-start | bytes 8912896 | tf_op jit(solution)/shard_map/all_gather | solution.py:112
  9.3 9.5 %copy-start.13 = (s32[2048,2]{0,1:T(2,128)S(1)}, s32[2048,2]{0,1:T(2,128)}, u32[]{:S(2)}) copy-start(s32[2048,2]{0,1:T(2,128)} %param.26) | copy-start | bytes 49156
  13.8 7.9 %copy-start.24 = (s32[1,4]{1,0:T(1,128)S(1)}, s32[1,4]{1,0:T(1,128)}, u32[]{:S(2)}) copy-start(s32[1,4]{1,0:T(1,128)} %param.25) | copy-start | bytes 52
  13.8 26.8 %all-to-all-start = ((bf16[8,128,1,256]{3,1,2,0:T(8,128)(2,1)}), bf16[8,128,1,256]{3,1,2,0:T(8,128)(2,1)}, u32[]{:S(2)}, u32[]{:S(2)}) async-start(bf16[8,128,1,256]{3,1,2,0:T(8,128)(2,1)} %copy.128), calls=%async_computation | async-start | bytes 1048576 | tf_op jit(solution)/shard_map/all_to_all | solution.py:99
  18.7 256.5 %reduce-scatter.2.cloned.1.call-start = ((), (), s32[]{:S(2)}) async-start(), calls=%async_computation.5 | async-start | bytes 8912896 | tf_op jit(solution)/shard_map/reduce_scatter | solution.py:164
  31.0 3.3 copy-start.15
  32.5 8.1 %copy-start.10 = (s32[2048]{0:T(1024)}, s32[2048]{0:T(1024)S(1)}, u32[]{:S(2)}) copy-start(s32[2048]{0:T(1024)S(1)} %convert_reduce_fusion.1) | copy-start | bytes 24580
  34.3 50.4 %copy-start.8 = (bf16[256,2048]{1,0:T(8,128)(2,1)S(1)}, bf16[256,2048]{1,0:T(8,128)(2,1)}, u32[]{:S(2)}) copy-start(bf16[256,2048]{1,0:T(8,128)(2,1)} %copy.130) | copy-start | bytes 3145732
  35.7 6.7 %copy-start.19 = (f32[64]{0:T(128)}, f32[64]{0:T(128)S(1)}, u32[]{:S(2)}) copy-start(f32[64]{0:T(128)S(1)} %multiply_power_fusion) | copy-start | bytes 772
  36.6 5.8 %copy-start.11 = (f32[2048]{0:T(1024)}, f32[2048]{0:T(1024)S(1)}, u32[]{:S(2)}) copy-start(f32[2048]{0:T(1024)S(1)} %subtract_convert_fusion.1) | copy-start | bytes 24580
  84.6 7.8 %copy-start.22 = (bf16[2048,2048]{1,0:T(8,128)(2,1)S(1)}, bf16[2048,2048]{1,0:T(8,128)(2,1)}, u32[]{:S(2)}) copy-start(bf16[2048,2048]{1,0:T(8,128)(2,1)} %all-gather.3.cloned.1.call-done) | copy-start | bytes 25165828
  90.6 2.0 copy-start.5
  92.5 4.5 %copy-start.3 = (f32[2048,64]{0,1:T(8,128)S(1)}, f32[2048,64]{0,1:T(8,128)}, u32[]{:S(2)}) copy-start(f32[2048,64]{0,1:T(8,128)} %get-tuple-element.159) | copy-start | bytes 1572868
  92.5 4.5 %copy-start.4 = (f32[2048,64]{0,1:T(8,128)S(1)}, f32[2048,64]{0,1:T(8,128)}, u32[]{:S(2)}) copy-start(f32[2048,64]{0,1:T(8,128)} %get-tuple-element.160) | copy-start | bytes 1572868
  105.3 5.5 %copy-start.6 = (bf16[2048,1,128]{0,2,1:T(8,128)(2,1)S(1)}, bf16[2048,1,128]{0,2,1:T(8,128)(2,1)}, u32[]{:S(2)}) copy-start(bf16[2048,1,128]{0,2,1:T(8,128)(2,1)} %fusion.52) | copy-start | bytes 1572868
  111.9 4.7 %copy-start.14 = (s32[4096]{0:T(1024)S(1)}, s32[4096]{0:T(1024)}, u32[]{:S(2)}) copy-start(s32[4096]{0:T(1024)} %broadcast_clamp_fusion) | copy-start | bytes 49156
  116.6 13.0 %copy-start.16 = (pred[4,1024]{1,0:T(4,128)(4,1)S(1)}, pred[4,1024]{1,0:T(4,128)(4,1)}, u32[]{:S(2)}) copy-start(pred[4,1024]{1,0:T(4,128)(4,1)} %compare_and_fusion) | copy-start | bytes 12292
  116.6 15.1 %copy-start.17 = (s32[2560]{0:T(1024)S(1)}, s32[2560]{0:T(1024)}, u32[]{:S(2)}) copy-start(s32[2560]{0:T(1024)} %pad_add_fusion) | copy-start | bytes 30724
  116.6 15.1 %copy-start.25 = (s32[2560]{0:T(1024)S(1)}, s32[2560]{0:T(1024)}, u32[]{:S(2)}) copy-start(s32[2560]{0:T(1024)} %constant.115.clone.1) | copy-start | bytes 30724
  131.7 36.9 %copy-start.7 = (s32[2048,2]{1,0:T(8,128)S(1)}, s32[2048,2]{1,0:T(8,128)}, u32[]{:S(2)}) copy-start(s32[2048,2]{1,0:T(8,128)} %copy.119) | copy-start | bytes 49156
  136.6 1.6 copy-start.9
  189.5 85.7 %copy-start.1 = (bf16[128,2048]{1,0:T(8,128)(2,1)S(1)}, bf16[128,2048]{1,0:T(8,128)(2,1)}, u32[]{:S(2)}) copy-start(bf16[128,2048]{1,0:T(8,128)(2,1)} %param.18) | copy-start | bytes 1572868
  189.5 87.0 %copy-start.12 = (f32[1,2048]{1,0:T(1,128)S(1)}, f32[1,2048]{1,0:T(1,128)}, u32[]{:S(2)}) copy-start(f32[1,2048]{1,0:T(1,128)} %get-tuple-element.158) | copy-start | bytes 24580
  189.6 204.8 %all-gather.5.cloned.1.call-start = ((), (), s32[]{:S(2)}) async-start(), calls=%async_computation.6 | async-start | bytes 8912896 | tf_op jit(solution)/shard_map/all_gather | solution.py:113
  278.5 57.4 %slice-start = ((s8[5767168]{0:T(1024)(128)(4,1)}), s8[4194304]{0:T(1024)(128)(4,1)S(1)}, s32[]{:S(2)}) async-start(s8[5767168]{0:T(1024)(128)(4,1)} %bitcast.194), calls=%async_computation.7 | async-start | bytes 8388608
  323.5 12.4 %slice-start.1 = ((s8[5767168]{0:T(1024)(128)(4,1)}), s8[1572864]{0:T(1024)(128)(4,1)S(1)}, s32[]{:S(2)}) async-start(s8[5767168]{0:T(1024)(128)(4,1)} %bitcast.194), calls=%async_computation.8 | async-start | bytes 3145728
  342.0 6.9 %copy-start.20 = (f32[128,2]{0,1:T(2,128)S(1)}, f32[128,2]{0,1:T(2,128)}, u32[]{:S(2)}) copy-start(f32[128,2]{0,1:T(2,128)} %param.31) | copy-start | bytes 3076
  342.0 7.8 %copy-start.21 = (s32[32]{0:T(128)S(1)}, s32[32]{0:T(128)}, u32[]{:S(2)}) copy-start(s32[32]{0:T(128)} %param.33) | copy-start | bytes 388
  342.0 57.2 %all-to-all-start.2 = ((bf16[16,40,2048]{2,1,0:T(8,128)(2,1)}), bf16[16,40,2048]{2,1,0:T(8,128)(2,1)}, u32[]{:S(2)}, u32[]{:S(2)}) async-start(bf16[16,40,2048]{2,1,0:T(8,128)(2,1)} %fusion.21), calls=%async_computation.3 | async-start | bytes 5242880 | tf_op jit(solution)/shard_map/all_to_all | solution.py:194
  412.2 6.6 %copy-start.2 = (bf16[128,2048]{1,0:T(8,128)(2,1)S(1)}, bf16[128,2048]{1,0:T(8,128)(2,1)}, u32[]{:S(2)}) copy-start(bf16[128,2048]{1,0:T(8,128)(2,1)} %reduce-scatter.2.cloned.1.call-done) | copy-start | bytes 1572868
  (4 other events, 5.5 us)
Sparse Core Ops, SparseCore 0:
  11.5 73.1 all-gather.2
  189.7 85.4 reduce-scatter.1
  277.3 116.9 all-gather.4
where the time goes:
time: 434 us; the launch traced here: 429 us
  waiting for transfers between devices  170 us (39%)
  matrix products  82.2 us (19%)
  local copies, waits for them, and re-layouts  64.2 us (15%)
  blocking collectives  45 us (10%)
  other arithmetic  41.6 us (10%)
  between operations  13.9 us (3%)
  starting transfers between devices  11.4 us (3%)
    reduce_scatter x1, waiting for transfers between devices, on_device(): lax.psum_scatter(jnp.dot(flat_mixed, flat_out, preferred_element_type=jnp...  83.3 us
    all_to_all x1, blocking collectives, on_device(): lax.all_to_all(spread_rows, 'exp', split_axis=0, concat_axis=0, tiled=True)  45 us
    all_gather x1, waiting for transfers between devices, on_device(): lax.all_gather(adapters, 'exp', axis=0, tiled=True)  44.4 us
    all_gather x1, waiting for transfers between devices, on_device(): lax.all_gather(normed, 'exp', axis=0, tiled=True)  41.9 us
    dot_general x4, matrix products, attend_block(): jnp.einsum('qhd,khd->hqk', queries, key_rows, preferred_element_type=jnp....  16 us
    dot_general x1, matrix products, on_device(): jnp.einsum('tje,tjx->tex', slot_weights, heads_out.astype(jnp.float32), p...  14.3 us
    gather x1, local copies, waits for them, and re-layouts, on_device(): jnp.take(queries.reshape(group_rows * AEXP, local_heads * HD), chosen_row...  12.9 us
    dot_general x1, matrix products, on_device(): jnp.einsum('nd,dkf->nkf', flat_rows, w_in, preferred_element_type=jnp.flo...  11.9 us
  transfers between devices with their start and end apart: 5, of which 3 were waited for; matrix products, arithmetic and copies ran while one was open for 13% of the time, Pallas kernels for 0%

commit v1 on v0

v1 whole, which is shorter than its diff:
```python
import math

import jax
import jax.numpy as jnp
import numpy as np
from jax import lax
from jax.experimental import pallas as pl
from jax.experimental.pallas import tpu as pltpu
from jax.sharding import PartitionSpec as P

HD = 128
AEXP = 4
EXPERTS = 8
CACHE = 128
CAP = 40
SIDE = 4
MESH = pl.DeviceIdType.MESH
F32, BF16, I32 = jnp.float32, jnp.bfloat16, jnp.int32

norm_eps = 1e-05


def rms_scale(values, gain):
    values = values.astype(F32)
    factor = lax.rsqrt(jnp.mean(values * values, axis=-1, keepdims=True) + norm_eps)
    return (values * factor * gain).astype(BF16)


def place():
    me = lax.axis_index("exp")
    return me, lax.div(me, SIDE), lax.rem(me, SIDE)


def beside(y, z, axis, step):
    if axis == 0:
        return lax.rem(y + step, SIDE) * SIDE + z
    return y * SIDE + lax.rem(z + step, SIDE)


def shard_at(y, z, half, first, second):
    if half == 0:
        return lax.rem(y + first, SIDE) * SIDE + lax.rem(z + second, SIDE)
    return lax.rem(y + second, SIDE) * SIDE + lax.rem(z + first, SIDE)


def meet_neighbours(y, z):
    barrier = pltpu.get_barrier_semaphore()
    for axis in (0, 1):
        for step in (1, 3):
            pl.semaphore_signal(
                barrier, inc=1, device_id={"exp": beside(y, z, axis, step)}, device_id_type=MESH
            )
    return barrier


class Sender:
    def __init__(self, y, z, sems):
        self.y, self.z, self.sems, self.sent = y, z, sems, []

    def copy(self, src, dst, recv, axis, step, slot):
        return pltpu.make_async_remote_copy(
            src_ref=src,
            dst_ref=dst,
            send_sem=self.sems.at[slot],
            recv_sem=recv,
            device_id={"exp": beside(self.y, self.z, axis, step)},
            device_id_type=MESH,
        )

    def send(self, src, dst, recv, axis, step):
        done = self.copy(src, dst, recv, axis, step, len(self.sent))
        done.start()
        self.sent.append(done)

    def arrive(self, dst, recv):
        self.copy(dst, dst, recv, 0, 1, 0).wait_recv()

    def finish(self):
        for done in self.sent:
            done.wait_send()


def ends_of(lens):
    ends, total = [], 0
    for r in range(4):
        total = total + lens[r]
        ends.append(total)
    return ends


def start_of(rows, ends):
    begin = jnp.zeros_like(rows)
    for end in ends[:3]:
        begin = jnp.where(rows >= end, end, begin)
    return begin


def project_kernel(
    lens, tok, gain, wq, wkv, freq, ids, q_out, k_out, v_out, held, w, acc, idt, ssem, rsem
):
    me, y, z = place()
    barrier = meet_neighbours(y, z)
    held[me] = rms_scale(tok[...], gain[0:1]).reshape(4, 32, -1)
    pl.semaphore_wait(barrier, 4)
    link = Sender(y, z, ssem)

    def send(s, piece, axis, step):
        link.send(held.at[s, piece], held.at[s, piece], rsem.at[s, piece], axis, step)

    def arrive(s, half):
        for p in (0, 1):
            link.arrive(held.at[s, 2 * half + p], rsem.at[s, 2 * half + p])

    for second in (0, 1):
        for half in (0, 1):
            for p in (0, 1):
                for step in (1, 3):
                    send(me, 2 * half + p, (half + second) % 2, step)

    rows256 = lax.broadcasted_iota(I32, (256, 256), 0)
    cols256 = lax.broadcasted_iota(I32, (256, 256), 1)
    by4 = (cols256 == lax.rem(rows256, 64) * 4 + lax.div(rows256, 64)).astype(BF16)
    by2 = (cols256 == lax.rem(rows256, 128) * 2 + lax.div(rows256, 128)).astype(BF16)

    def split4(b, carry):
        part = jnp.dot(by4, wq[pl.ds(b * 256, 256), :], preferred_element_type=F32).astype(BF16)
        for e in range(4):
            w[pl.ds(b * 64, 64), e * HD : (e + 1) * HD] = part[e * 64 : (e + 1) * 64]
        return carry

    def split2(b, carry):
        part = jnp.dot(by2, wkv[pl.ds(b * 256, 256), :], preferred_element_type=F32).astype(BF16)
        for e in range(2):
            w[pl.ds(b * 128, 128), (4 + e) * HD : (5 + e) * HD] = part[e * 128 : (e + 1) * 128]
        return carry

    lax.fori_loop(0, 32, split4, 0)
    lax.fori_loop(0, 16, split2, 0)

    def turn_ids(b, carry):
        at = pl.ds(pl.multiple_of(b * 128, 128), 128)
        block = jnp.concatenate([ids[:, at], jnp.zeros((6, 128), I32)], axis=0)
        idt[at, :] = block.astype(F32).T
        return carry

    lax.fori_loop(0, 16, turn_ids, 0)
    ends = ends_of(lens)
    lane = lax.broadcasted_iota(I32, (256, HD), 1)

    def project(half, across):
        shards = [a * (4 - 3 * half) + across * (1 + 3 * half) for a in range(4)]
        lhs = jnp.concatenate(
            [held[s, pl.ds(2 * half, 2)].reshape(64, -1) for s in shards], axis=0
        )
        acc[...] = jnp.dot(lhs, w[...], preferred_element_type=F32)
        starts = [pl.multiple_of(s * 128 + half * 64, 64) for s in shards]
        rows = jnp.concatenate(
            [lax.broadcasted_iota(I32, (64, 1), 0) + at for at in starts], axis=0
        )
        places = CACHE + rows - start_of(rows, ends)
        angle = places.astype(F32) * freq[...]
        cosine = jnp.cos(angle)
        sine = jnp.sin(angle)
        sine = jnp.where(lane < HD // 2, -sine, sine)

        def turn(v):
            return (v * cosine + pltpu.roll(v, HD // 2, 1) * sine).astype(BF16)

        named = jnp.concatenate([idt[pl.ds(at, 64), :] for at in starts], axis=0)
        slots = []
        for j in (0, 1):
            pick = acc[:, 0:HD]
            for e in range(1, 4):
                pick = jnp.where(named[:, j : j + 1] == float(e), acc[:, e * HD : (e + 1) * HD], pick)
            slots.append(turn(pick))
        keys = turn(acc[:, 4 * HD : 5 * HD])
        values = acc[:, 5 * HD : 6 * HD].astype(BF16)
        for a in range(4):
            at, piece = pl.ds(starts[a], 64), slice(a * 64, (a + 1) * 64)
            q_out[at, 0:HD] = slots[0][piece]
            q_out[at, HD : 2 * HD] = slots[1][piece]
            k_out[at, :] = keys[piece]
            v_out[at, :] = values[piece]

    for half in (0, 1):
        for first, piece, step in ((3, 0, 1), (1, 1, 3)):
            s = shard_at(y, z, half, first, 0)
            arrive(s, half)
            send(s, 2 * half + piece, half, step)
            for p in (0, 1):
                for onward in (1, 3):
                    send(s, 2 * half + p, 1 - half, onward)
    for half in (0, 1):
        s = shard_at(y, z, half, 2, 0)
        arrive(s, half)
        for p in (0, 1):
            for onward in (1, 3):
                send(s, 2 * half + p, 1 - half, onward)

    def second_of(half):
        return z * (1 - half) + y * half

    def own_step(n, carry):
        project(n, second_of(n))
        return carry

    lax.fori_loop(0, 2, own_step, 0)
    for first in (0, 3, 1, 2):
        for half in (0, 1):
            for second, piece, step in ((3, 0, 1), (1, 1, 3)):
                s = shard_at(y, z, half, first, second)
                arrive(s, half)
                send(s, 2 * half + piece, 1 - half, step)

    def near_step(n, carry):
        half = lax.div(n, 2)
        project(half, lax.rem(second_of(half) + 1 + 2 * lax.rem(n, 2), SIDE))
        return carry

    lax.fori_loop(0, 4, near_step, 0)
    for half in (0, 1):
        for first in (0, 3, 1, 2):
            arrive(shard_at(y, z, half, first, 2), half)

    def far_step(n, carry):
        project(n, lax.rem(second_of(n) + 2, SIDE))
        return carry

    lax.fori_loop(0, 2, far_step, 0)
    link.finish()


def project(tokens, norm_gains, wq, wkv, lens, ids):
    rows = tokens.shape[0] * 16
    width = tokens.shape[1]
    lanes = np.arange(HD) % (HD // 2)
    freq = np.power(10000.0, lanes * (-2.0 / HD)).astype(np.float32)[None, :]
    vmem = pl.BlockSpec(memory_space=pltpu.VMEM)
    return pl.pallas_call(
        project_kernel,
        out_shape=(
            jax.ShapeDtypeStruct((rows, 2 * HD), BF16),
            jax.ShapeDtypeStruct((rows, HD), BF16),
            jax.ShapeDtypeStruct((rows, HD), BF16),
        ),
        in_specs=[pl.BlockSpec(memory_space=pltpu.SMEM)] + [vmem] * 6,
        out_specs=(vmem, vmem, vmem),
        scratch_shapes=[
            pltpu.VMEM((16, 4, 32, width), BF16),
            pltpu.VMEM((width, 6 * HD), BF16),
            pltpu.VMEM((256, 6 * HD), F32),
            pltpu.VMEM((rows, 8), F32),
            pltpu.SemaphoreType.DMA((60,)),
            pltpu.SemaphoreType.DMA((16, 4)),
        ],
        compiler_params=pltpu.CompilerParams(collective_id=0, has_side_effects=True),
        name="gather_project",
    )(lens, tokens, norm_gains, wq, wkv, jnp.asarray(freq), ids)


def attend_kernel(lens, sender, q, k, v, pages, ids, gates, out, acc):
    block = pl.program_id(0)
    ends = ends_of(lens)
    first = block * 128
    last = first + 127
    scale = 1.0 / math.sqrt(HD)
    queries = jnp.concatenate([q[:, 0:HD], q[:, HD : 2 * HD]], axis=0)
    rows = lax.broadcasted_iota(I32, (128, 1), 0) + first
    rows = jnp.concatenate([rows, rows], axis=0)
    begin = start_of(rows, ends)
    low, high, low_start = 0, 0, 0
    for end in ends[:3]:
        low = low + (first >= end).astype(I32)
        high = high + (last >= end).astype(I32)
        low_start = jnp.where(first >= end, end, low_start)
    acc[...] = jnp.zeros_like(acc)

    def fold(state, keys, values, visible):
        top, total = state
        scores = lax.dot_general(
            queries, keys, (((1,), (1,)), ((), ())), preferred_element_type=F32
        )
        scores = jnp.where(visible, scores * scale, -1e30)
        peak = jnp.maximum(top, jnp.max(scores, axis=-1, keepdims=True))
        kept = jnp.exp(top - peak)
        raised = jnp.exp(scores - peak)
        acc[...] = acc[...] * kept + jnp.dot(
            raised.astype(BF16), values, preferred_element_type=F32
        )
        return peak, total * kept + jnp.sum(raised, axis=-1, keepdims=True)

    def cached_step(r, state):
        begins = jnp.where(r == 0, 0, jnp.where(r == 1, ends[0], jnp.where(r == 2, ends[1], ends[2])))
        came = sender[r]
        page = pages[came]
        mine = jnp.broadcast_to(begin == begins, (256, CACHE))
        return fold(state, page[:, 0:HD], page[:, HD : 2 * HD], mine)

    def key_step(b, state):
        at = pl.ds(pl.multiple_of(b * 256, 256), 256)
        cols = lax.broadcasted_iota(I32, (256, 256), 1) + b * 256
        return fold(state, k[at, :], v[at, :], (cols >= begin) & (cols <= rows))

    state = (jnp.full((256, 1), -1e30, F32), jnp.zeros((256, 1), F32))
    state = lax.fori_loop(low, high + 1, cached_step, state)
    state = lax.fori_loop(lax.div(low_start, 256), lax.div(last, 256) + 1, key_step, state)
    heads = (acc[...] / state[1]).astype(BF16).astype(F32)
    named = jnp.concatenate([ids[...], jnp.zeros((6, 128), I32)], axis=0).astype(F32).T
    weight = jnp.concatenate([gates[...], jnp.zeros((6, 128), F32)], axis=0).T
    for e in range(AEXP):
        mixed = jnp.zeros((128, HD), F32)
        for j in (0, 1):
            part = heads[j * 128 : (j + 1) * 128] * weight[:, j : j + 1]
            mixed = mixed + jnp.where(named[:, j : j + 1] == float(e), part, 0.0)
        out[:, e * HD : (e + 1) * HD] = mixed.astype(BF16)


def attend(q, k, v, pages, lens, sender, ids, gates):
    rows = q.shape[0]
    smem = pl.BlockSpec(memory_space=pltpu.SMEM)
    return pl.pallas_call(
        attend_kernel,
        out_shape=jax.ShapeDtypeStruct((rows, AEXP * HD), BF16),
        grid=(rows // 128,),
        in_specs=[
            smem,
            smem,
            pl.BlockSpec((128, 2 * HD), lambda i: (i, 0)),
            pl.BlockSpec((rows, HD), lambda i: (0, 0)),
            pl.BlockSpec((rows, HD), lambda i: (0, 0)),
            pl.BlockSpec(pages.shape, lambda i: (0, 0, 0)),
            pl.BlockSpec((2, 128), lambda i: (0, i)),
            pl.BlockSpec((2, 128), lambda i: (0, i)),
        ],
        out_specs=pl.BlockSpec((128, AEXP * HD), lambda i: (i, 0)),
        scratch_shapes=[pltpu.VMEM((256, HD), F32)],
        name="attend_mix",
    )(lens, sender, q, k, v, pages, ids, gates)


ORDER = (2, 1, 3, 0)


def reduce_kernel(
    mixed, w, tok, gain, hidden, hnorm, far, near, own, rx_far, rx_near, far2, near2, rx_far2, rx_near2,
    ssem, far_sem, near_sem, far2_sem, near2_sem,
):
    me, y, z = place()
    barrier = meet_neighbours(y, z)
    link = Sender(y, z, ssem)

    def partial(half, first):
        one = lax.rem(y * (1 - half) + z * half + first, SIDE)
        parts = []
        for offset in ORDER:
            two = lax.rem(z * (1 - half) + y * half + offset, SIDE)
            s = one * (4 - 3 * half) + two * (1 + 3 * half)
            parts.append(mixed[pl.ds(pl.multiple_of(s * 128 + half * 64, 64), 64), :])
        return jnp.dot(jnp.concatenate(parts, axis=0), w[...], preferred_element_type=F32)

    def far_step(half, carry):
        far[half] = partial(half, 2).astype(BF16).reshape(far.shape[1:])
        return carry

    lax.fori_loop(0, 2, far_step, 0)
    pl.semaphore_wait(barrier, 4)
    for i in range(4):
        for half in (0, 1):
            for p in (0, 1):
                link.send(
                    far.at[half, i, p], rx_far.at[half, p, i], far_sem.at[half, p, i], half, 1 + 2 * p
                )

    def near_step(n, carry):
        half, way = lax.div(n, 2), lax.rem(n, 2)
        near[half, way] = partial(half, 1 + 2 * way).astype(BF16).reshape(near.shape[2:])
        return carry

    lax.fori_loop(0, 4, near_step, 0)

    def send_near(half, way, i, p):
        link.send(
            near.at[half, way, i, p],
            rx_near.at[half, way, i, p],
            near_sem.at[half, way, i, p],
            half,
            1 + 2 * way,
        )

    for i in range(4):
        for half in (0, 1):
            for way in (0, 1):
                send_near(half, way, i, 1 - way)

    def own_step(half, carry):
        own[half] = partial(half, 0).reshape(own.shape[1:])
        return carry

    lax.fori_loop(0, 2, own_step, 0)

    for i in range(4):
        for half in (0, 1):
            for way in (0, 1):
                link.arrive(rx_far.at[half, way, i], far_sem.at[half, way, i])
                near[half, way, i, way] = (
                    near[half, way, i, way].astype(F32) + rx_far[half, way, i].astype(F32)
                ).astype(BF16)
        for half in (0, 1):
            for way in (0, 1):
                send_near(half, way, i, way)

    def total(half, i):
        for way in (0, 1):
            for p in (0, 1):
                link.arrive(rx_near.at[half, way, i, p], near_sem.at[half, way, i, p])
        summed = own[half, i]
        for way in (0, 1):
            summed = summed + rx_near[half, way, i].astype(F32)
        return summed

    def send_near2(half, way, p):
        link.send(
            near2.at[half, way, p],
            rx_near2.at[half, way, p],
            near2_sem.at[half, way, p],
            1 - half,
            1 + 2 * way,
        )

    for half in (0, 1):
        far2[half] = total(half, 0).astype(BF16)
    for half in (0, 1):
        for p in (0, 1):
            link.send(far2.at[half, p], rx_far2.at[half, p], far2_sem.at[half, p], 1 - half, 1 + 2 * p)
    for way in (0, 1):
        for half in (0, 1):
            near2[half, way] = total(half, 1 + way).astype(BF16)
        for half in (0, 1):
            send_near2(half, way, 1 - way)
    for way in (0, 1):
        for half in (0, 1):
            link.arrive(rx_far2.at[half, way], far2_sem.at[half, way])
            near2[half, way, way] = (
                near2[half, way, way].astype(F32) + rx_far2[half, way].astype(F32)
            ).astype(BF16)
        for half in (0, 1):
            send_near2(half, way, way)
    for half in (0, 1):
        own[half, 3] = total(half, 3)
    for half in (0, 1):
        summed = own[half, 3]
        for way in (0, 1):
            for p in (0, 1):
                link.arrive(rx_near2.at[half, way, p], near2_sem.at[half, way, p])
            summed = summed + rx_near2[half, way].astype(F32)
        rows = slice(half * 64, (half + 1) * 64)
        state = (tok[rows, :].astype(F32) + summed.reshape(64, -1)).astype(BF16)
        hidden[rows, :] = state
        hnorm[rows, :] = rms_scale(state, gain[1:2])
    link.finish()


def reduce_out(mixed, w_out, tokens, norm_gains):
    width = tokens.shape[1]
    vmem = pl.BlockSpec(memory_space=pltpu.VMEM)
    shape = jax.ShapeDtypeStruct(tokens.shape, BF16)
    piece = (32, width)
    dma = pltpu.SemaphoreType.DMA
    return pl.pallas_call(
        reduce_kernel,
        out_shape=(shape, shape),
        in_specs=[vmem] * 4,
        out_specs=(vmem, vmem),
        scratch_shapes=[
            pltpu.VMEM((2, 4, 2) + piece, BF16),
            pltpu.VMEM((2, 2, 4, 2) + piece, BF16),
            pltpu.VMEM((2, 4, 2) + piece, F32),
            pltpu.VMEM((2, 2, 4) + piece, BF16),
            pltpu.VMEM((2, 2, 4, 2) + piece, BF16),
            pltpu.VMEM((2, 2) + piece, BF16),
            pltpu.VMEM((2, 2, 2) + piece, BF16),
            pltpu.VMEM((2, 2) + piece, BF16),
            pltpu.VMEM((2, 2, 2) + piece, BF16),
            dma((60,)),
            dma((2, 2, 4)),
            dma((2, 2, 4, 2)),
            dma((2, 2)),
            dma((2, 2, 2)),
        ],
        compiler_params=pltpu.CompilerParams(collective_id=1, has_side_effects=True),
        name="project_reduce",
    )(mixed, w_out, tokens, norm_gains)


def on_device(
    tokens,
    norm_gains,
    w_query,
    w_keyval,
    w_out,
    page_pool,
    page_dest,
    prompt_lens,
    att_ids,
    att_gates,
    w_in,
    w_down,
    moe_ids,
    moe_gates,
    adapters,
    req_adapter,
):
    groups = lax.axis_size("req")
    columns = lax.axis_size("exp")
    group_index = lax.axis_index("req")
    column_index = lax.axis_index("exp")
    tok_rows, width = tokens.shape
    slot_count = page_pool.shape[0]
    group_numbers = jnp.arange(groups, dtype=I32)
    lens = prompt_lens.reshape(-1)

    own_target = (
        lax.dynamic_slice_in_dim(page_dest, group_index * slot_count, slot_count) // slot_count
    )
    slot_for = jnp.sum(
        jnp.where(
            own_target[None, :] == group_numbers[:, None],
            jnp.arange(slot_count, dtype=I32)[None, :],
            0,
        ),
        axis=1,
    )
    outgoing = jnp.take(page_pool.reshape(slot_count, CACHE, 2 * HD), slot_for, axis=0)
    pages = lax.all_to_all(outgoing, "req", split_axis=0, concat_axis=0, tiled=True)
    pool_slots = jnp.arange(page_dest.shape[0], dtype=I32)
    wanted = group_index * slot_count + jnp.arange(slot_count, dtype=I32)
    sender = (
        jnp.sum(jnp.where(page_dest[None, :] == wanted[:, None], pool_slots[None, :], 0), axis=1)
        // slot_count
    )

    wanted_ids = lax.dynamic_slice_in_dim(req_adapter, group_index * slot_count, slot_count)
    local_ids = wanted_ids - column_index * adapters.shape[0]
    held_here = (local_ids >= 0) & (local_ids < adapters.shape[0])
    share = jnp.where(
        held_here[:, None, None, None],
        jnp.take(adapters, jnp.clip(local_ids, 0, adapters.shape[0] - 1), axis=0),
        jnp.zeros((), BF16),
    )
    share = share.reshape(columns, -1, width)
    pieces = lax.all_to_all(share, "exp", split_axis=0, concat_axis=0, tiled=True)
    whole = jnp.sum(pieces.astype(F32), axis=0).astype(BF16)
    spread = jnp.broadcast_to(whole[None], share.shape)
    group_factors = lax.all_to_all(spread, "exp", split_axis=0, concat_axis=0, tiled=True)
    group_factors = group_factors.reshape(slot_count, *adapters.shape[1:])

    ids = att_ids.T
    q, k, v = project(
        tokens,
        norm_gains,
        w_query.reshape(width * AEXP, HD),
        w_keyval.reshape(width * 2, HD),
        lens,
        ids,
    )
    mixed = attend(q, k, v, pages, lens, sender, ids, att_gates.T)
    hidden_state, hnorm = reduce_out(mixed, w_out.reshape(-1, width), tokens, norm_gains)

    expert_flat = moe_ids.reshape(-1)
    expert_hits = (expert_flat[:, None] == jnp.arange(EXPERTS, dtype=I32)[None, :]).astype(I32)
    earlier = jnp.cumsum(expert_hits, axis=0) - expert_hits
    route_slot = jnp.sum(earlier * expert_hits, axis=1) + expert_flat * CAP
    table_size = EXPERTS * CAP
    placing = (jnp.arange(table_size, dtype=I32)[:, None] == route_slot[None, :]).reshape(
        table_size, tok_rows, 2
    )
    placing = jnp.any(placing, axis=2).astype(BF16)
    packed = jnp.dot(placing, hnorm, preferred_element_type=F32).astype(BF16)
    packed = packed.reshape(EXPERTS, CAP, width)
    copies = columns // EXPERTS
    spread_rows = jnp.repeat(packed, copies, axis=0)
    arrived = lax.all_to_all(spread_rows, "exp", split_axis=0, concat_axis=0, tiled=True)
    flat_rows = arrived.reshape(-1, width)
    gate_up = jnp.einsum("nd,dkf->nkf", flat_rows, w_in, preferred_element_type=F32)
    inner_act = (jax.nn.silu(gate_up[:, 0]) * gate_up[:, 1]).astype(BF16)
    partial_out = jnp.dot(inner_act, w_down, preferred_element_type=F32).reshape(
        columns, CAP, width
    )
    returned = lax.all_to_all(
        partial_out.astype(BF16), "exp", split_axis=0, concat_axis=0, tiled=True
    ).astype(F32)
    summed = jnp.sum(returned.reshape(EXPERTS, copies, CAP, width), axis=1).reshape(
        table_size, width
    )
    routed_rows = jnp.take(summed, route_slot, axis=0).reshape(tok_rows, 2, width)
    expert_out = jnp.sum(routed_rows * moe_gates[:, :, None], axis=1)
    own_rows = column_index * tok_rows + jnp.arange(tok_rows, dtype=I32)
    own_segment = jnp.sum((own_rows[:, None] >= jnp.cumsum(lens)[None, :]).astype(I32), axis=1)
    lowrank = jnp.einsum("td,qrd->tqr", hnorm, group_factors[:, 0], preferred_element_type=F32)
    member = own_segment[:, None] == jnp.arange(slot_count, dtype=I32)[None, :]
    lowrank = jnp.where(member[:, :, None], lowrank, 0.0).astype(BF16)
    delta = jnp.einsum("tqr,qrd->td", lowrank, group_factors[:, 1], preferred_element_type=F32)
    return (hidden_state.astype(F32) + expert_out + delta).astype(BF16)


def solution(mesh):
    in_specs = (
        P(("req", "exp"), None),
        P(),
        P(None, None, "exp"),
        P(None, None, "exp"),
        P(None, "exp", None),
        P("req", None, "exp", None),
        P(),
        P("req", None),
        P("req", None),
        P("req", None),
        P(None, None, "exp"),
        P("exp", None),
        P(("req", "exp"), None),
        P(("req", "exp"), None),
        P("exp", None, None, None),
        P(),
    )
    out_specs = P(("req", "exp"), None)
    return jax.shard_map(
        on_device, mesh=mesh, in_specs=in_specs, out_specs=out_specs, check_vma=False
    )
```

time: 434 us -> 290 us (0.67)
  Pallas kernels: 0 us -> 143 us
  waiting for transfers between devices: 170 us -> 60.5 us
  matrix products: 82.2 us -> 24.8 us
  local copies, waits for them, and re-layouts: 64.2 us -> 14.6 us
  blocking collectives: 45 us -> 0 us
  other arithmetic: 41.6 us -> 13.5 us
  starting transfers between devices: 11.4 us -> 32.4 us
  between operations: 13.9 us -> 0.19 us
    pallas_call x0 -> x3, Pallas kernels: none -> 143 us  [the longest x1 57.6 us: project(): pl.pallas_call(project_kernel, out_shape=(jax.ShapeDtypeStruct((rows, 2 *...]
    all_gather x2 -> x0, waiting for transfers between devices: 86.4 us -> none  [the longest x1 44.4 us: on_device(): lax.all_gather(adapters, 'exp', axis=0, tiled=True)]
    reduce_scatter x1 -> x0, waiting for transfers between devices: 83.3 us -> none  [on_device(): lax.psum_scatter(jnp.dot(flat_mixed, flat_out, preferred_element_type=jnp...]
    all_to_all x1 -> x4, waiting for transfers between devices: 0.01 us -> 60.5 us  [the longest x1 30.3 us: on_device(): lax.all_to_all(partial_out.astype(BF16), 'exp', split_axis=0, concat_axis...]
    dot_general x17 -> x3, matrix products: 79.1 us -> 21.6 us  [the longest x1 11.7 us: on_device(): jnp.einsum('nd,dkf->nkf', flat_rows, w_in, preferred_element_type=F32)]
    all_to_all x1 -> x0, blocking collectives: 45 us -> none  [on_device(): lax.all_to_all(spread_rows, 'exp', split_axis=0, concat_axis=0, tiled=True)]
    all_to_all x1 -> x4, starting transfers between devices: 6.48 us -> 27.5 us  [the longest x1 7.37 us: on_device(): lax.all_to_all(partial_out.astype(BF16), 'exp', split_axis=0, concat_axis...]
    gather x2, local copies, waits for them, and re-layouts: 16.9 us -> 2.9 us  [the longest x1 1.53 us: on_device(): jnp.take(page_pool.reshape(slot_count, CACHE, 2 * HD), slot_for, axis=0)]
  transfers between devices with their start and end apart: 5 -> 5, of which waited for: 3 -> 2; matrix products, arithmetic and copies ran while one was open for 13% -> 14% of each run, Pallas kernels for 0% -> 20%
where the time goes in v1:
time: 290 us; the launch traced here: 289 us
  Pallas kernels  143 us (49%)
  waiting for transfers between devices  60.5 us (21%)
  starting transfers between devices  32.4 us (11%)
  matrix products  24.8 us (9%)
  local copies, waits for them, and re-layouts  14.6 us (5%)
  other arithmetic  13.5 us (5%)
    pallas_call x1, Pallas kernels, project(): pl.pallas_call(project_kernel, out_shape=(jax.ShapeDtypeStruct((rows, 2 *...  57.6 us
    pallas_call x1, Pallas kernels, reduce_out(): pl.pallas_call(reduce_kernel, out_shape=(shape, shape), in_specs=[vmem] *...  51.9 us
    pallas_call x1, Pallas kernels, attend(): pl.pallas_call(attend_kernel, out_shape=jax.ShapeDtypeStruct((rows, AEXP...  33.5 us
    all_to_all x1, waiting for transfers between devices, on_device(): lax.all_to_all(partial_out.astype(BF16), 'exp', split_axis=0, concat_axis...  30.3 us
    all_to_all x1, waiting for transfers between devices, on_device(): lax.all_to_all(spread_rows, 'exp', split_axis=0, concat_axis=0, tiled=True)  30.2 us
    dot_general x1, matrix products, on_device(): jnp.einsum('nd,dkf->nkf', flat_rows, w_in, preferred_element_type=F32)  11.7 us
    dot_general x1, matrix products, on_device(): jnp.dot(inner_act, w_down, preferred_element_type=F32)  8.38 us
    all_to_all x1, starting transfers between devices, on_device(): lax.all_to_all(partial_out.astype(BF16), 'exp', split_axis=0, concat_axis...  7.37 us
  transfers between devices with their start and end apart: 5, of which 2 were waited for; matrix products, arithmetic and copies ran while one was open for 14% of the time, Pallas kernels for 20%

profile of v1, /device:TPU:14, one launch (start us, length us, event | category | flops | bytes accessed | tf_op | source)
XLA Modules:
  0.0 288.9 jit_solution(6671176919144787647)
XLA Ops:
  0.0 0.8 and_select_fusion
  0.9 1.5 gather_fusion
  2.5 0.9 broadcast_select_fusion
  3.4 4.9 %all-to-all-start = ((bf16[8,128,256]{2,1,0:T(8,128)(2,1)}), bf16[8,128,256]{2,1,0:T(8,128)(2,1)S(1)}, u32[]{:S(2)}, u32[]{:S(2)}) async-start(bf16[8,128,256]{2,1,0:T(8,128)(2,1)} %broadcast_select_fusion), calls=%async_computation | async-start | bytes 1048576 | tf_op jit(solution)/shard_map/all_to_all | solution.py:534
  8.7 0.6 reduce-window.18
  9.3 0.2 slice_reduce_fusion
  9.9 57.6 %gather_project.1 = (bf16[2048,256]{1,0:T(8,128)(2,1)}, bf16[2048,128]{1,0:T(8,128)(2,1)}, bf16[2048,128]{1,0:T(8,128)(2,1)}) custom-call(s32[4]{0:T(128)} %bitcast.80, bf16[128,2048]{1,0:T(8,128)(2,1)} %tok.3, f32[2,2048]{1,0:T(2,128)} %gain.3, bf16[8192,128]{1,0:T(8,128)(2,1)} %bitcast.70, bf16[4096,128]{1,0:T(8,128)(2,1)} %bitcast.74, ...), custom_call_target="tpu_custom_call" | custom-call | tf_op jit(solution)/shard_map/gather_project/pallas_call | solution.py:239
  67.5 0.2 select_reduce_fusion.1
  67.7 0.5 and_select_fusion.1.sender
  68.2 0.8 copy-done.4
  69.0 33.5 %attend_mix.1.mixed = bf16[2048,512]{1,0:T(8,128)(2,1)} custom-call(s32[4]{0:T(128)} %bitcast.81, s32[4]{0:T(128)} %and_select_fusion.1.sender, bf16[2048,256]{1,0:T(8,128)(2,1)} %get-tuple-element.10.q, bf16[2048,128]{1,0:T(8,128)(2,1)} %get-tuple-element.11.k, bf16[2048,128]{1,0:T(8,128)(2,1)} %get-tuple-element.12.v, bf16[8,128,256]{2,1,0:T(8,128)(2,1)} %copy-done.4, ...), custom_call_target="tpu_custom_call" | custom-call | tf_op jit(solution)/shard_map/attend_mix/pallas_call | solution.py:321
  102.5 51.9 %project_reduce.1 = (bf16[128,2048]{1,0:T(8,128)(2,1)}, bf16[128,2048]{1,0:T(8,128)(2,1)}) custom-call(bf16[2048,512]{1,0:T(8,128)(2,1)} %attend_mix.1.mixed, bf16[512,2048]{1,0:T(8,128)(2,1)} %bitcast.71, bf16[128,2048]{1,0:T(8,128)(2,1)} %tok.3, f32[2,2048]{1,0:T(2,128)} %gain.3), custom_call_target="tpu_custom_call" | custom-call | tf_op jit(solution)/shard_map/project_reduce/pallas_call | solution.py:469
  154.4 1.5 convolution_convert_fusion
  156.0 1.8 broadcast_in_dim.120
  157.8 5.6 %all-to-all-start.1 = ((bf16[16,40,2048]{2,1,0:T(8,128)(2,1)}), bf16[16,40,2048]{2,1,0:T(8,128)(2,1)S(1)}, u32[]{:S(2)}, u32[]{:S(2)}) async-start(bf16[16,40,2048]{2,1,0:T(8,128)(2,1)} %bitcast.12), calls=%async_computation.1 | async-start | bytes 5242880 | tf_op jit(solution)/shard_map/all_to_all | solution.py:582
  163.8 1.4 gather_fusion.2
  165.2 2.0 select_select_fusion
  167.2 30.2 %all-to-all-done.1 = bf16[16,40,2048]{2,1,0:T(8,128)(2,1)S(1)} async-done(((bf16[16,40,2048]{2,1,0:T(8,128)(2,1)}), bf16[16,40,2048]{2,1,0:T(8,128)(2,1)S(1)}, u32[]{:S(2)}, u32[]{:S(2)}) %all-to-all-start.1) | async-done | bytes 2621472 | tf_op jit(solution)/shard_map/all_to_all | solution.py:582
  197.4 7.3 %all-to-all-start.3 = ((bf16[16,8,2048]{2,1,0:T(8,128)(2,1)}), bf16[16,8,2048]{2,1,0:T(8,128)(2,1)S(1)}, u32[]{:S(2)}, u32[]{:S(2)}) async-start(bf16[16,8,2048]{2,1,0:T(8,128)(2,1)} %select_select_fusion), calls=%async_computation.3 | async-start | bytes 1048576 | tf_op jit(solution)/shard_map/all_to_all | solution.py:551
  204.7 11.7 %fusion = f32[640,2,1408]{2,0,1:T(8,128)S(1)} fusion(bf16[640,2048,1]{1,0,2:T(8,128)(2,1)S(1)} %bitcast.69, bf16[2048,2,1408]{2,1,0:T(2,128)(2,1)} %param.27), kind=kOutput, calls=%fused_computation.3 | convolution fusion | flops 7381975040 | bytes 21364736 | tf_op jit(solution)/shard_map/nd,dkf->nkf/dot_general | solution.py:584
  216.4 0.5 fusion.24
  216.9 8.4 %fusion.4 = bf16[16,40,2048]{2,1,0:T(8,128)(2,1)} fusion(bf16[1408,2048]{1,0:T(8,128)(2,1)} %param.28, f32[16,40,1408]{2,1,0:T(8,128)S(1)} %bitcast.68, f32[16,40,1408]{2,1,0:T(8,128)S(1)} %bitcast.67), kind=kOutput, calls=%fused_computation.9 | convolution fusion | flops 3697704960 | bytes 15597568 | tf_op jit(solution)/shard_map/dot_general | solution.py:586
  225.3 7.4 %all-to-all-start.2 = ((bf16[16,40,2048]{2,1,0:T(8,128)(2,1)}), bf16[16,40,2048]{2,1,0:T(8,128)(2,1)S(1)}, u32[]{:S(2)}, u32[]{:S(2)}) async-start(bf16[16,40,2048]{2,1,0:T(8,128)(2,1)} %fusion.4), calls=%async_computation.2 | async-start | bytes 5242880 | tf_op jit(solution)/shard_map/all_to_all | solution.py:589
  233.5 30.3 %all-to-all-done.2 = bf16[16,40,2048]{2,1,0:T(8,128)(2,1)S(1)} async-done(((bf16[16,40,2048]{2,1,0:T(8,128)(2,1)}), bf16[16,40,2048]{2,1,0:T(8,128)(2,1)S(1)}, u32[]{:S(2)}, u32[]{:S(2)}) %all-to-all-start.2) | async-done | bytes 2621472 | tf_op jit(solution)/shard_map/all_to_all | solution.py:589
  263.8 0.9 broadcast_in_dim.132
  264.7 0.8 copy-done.2
  265.5 7.2 %all-to-all-start.4 = ((bf16[16,8,2048]{2,1,0:T(8,128)(2,1)}), bf16[16,8,2048]{2,1,0:T(8,128)(2,1)}, u32[]{:S(2)}, u32[]{:S(2)}) async-start(bf16[16,8,2048]{2,1,0:T(8,128)(2,1)} %broadcast_in_dim.132), calls=%async_computation.4 | async-start | bytes 1048576 | tf_op jit(solution)/shard_map/all_to_all | solution.py:554
  272.7 2.6 convert_reduce_fusion
  275.3 2.7 gather_fusion.1
  278.0 2.5 gather.18
  280.6 5.2 %multiply_reduce_fusion = f32[128,2048]{1,0:T(8,128)} fusion(f32[128,2,2048]{2,1,0:T(2,128)S(1)} %gather.18, pred[128,2]{1,0:T(8,128)(4,1)S(1)} %copy.39, f32[128,2]{1,0:T(8,128)S(1)} %copy.42), kind=kLoop, calls=%fused_computation.14 | loop fusion | flops 1310720 | bytes 3147008 | tf_op jit(solution)/shard_map/reduce_sum | solution.py:596
  285.8 3.2 %fusion.8 = bf16[128,2048]{1,0:T(8,128)(2,1)} fusion(f32[128,2048]{1,0:T(8,128)} %multiply_reduce_fusion, bf16[128,2048]{1,0:T(8,128)(2,1)} %get-tuple-element.13, bf16[128,2048]{1,0:T(8,128)(2,1)S(1)} %copy-done.3, bf16[4,2,16,2048]{3,2,1,0:T(8,128)(2,1)} %bitcast.26, pred[128,4]{0,1:T(4,128)(4,1)S(1)} %iota_compare_fusion.3), kind=kOutput, calls=%fused_computation.13 | convolution fusion | flops 68173824 | bytes 3146240 | tf_op jit(solution)/shard_map/tqr,qrd->td/dot_general | solution.py:602
  (55 shorter events, 2.2 us)
Async XLA Ops:
  0.0 163.8 %copy-start = (bf16[4,2,16,2048]{3,2,1,0:T(8,128)(2,1)S(1)}, bf16[4,2,16,2048]{3,2,1,0:T(8,128)(2,1)}, u32[]{:S(2)}) copy-start(bf16[4,2,16,2048]{3,2,1,0:T(8,128)(2,1)} %param.31) | copy-start | bytes 1572868
  0.0 8.3 %copy-start.5 = (s32[128,2]{0,1:T(2,128)S(1)}, s32[128,2]{0,1:T(2,128)}, u32[]{:S(2)}) copy-start(s32[128,2]{0,1:T(2,128)} %param.29) | copy-start | bytes 3076
  3.4 64.1 %copy-start.9 = (s32[32]{0:T(128)S(1)}, s32[32]{0:T(128)}, u32[]{:S(2)}) copy-start(s32[32]{0:T(128)} %param.23) | copy-start | bytes 388
  3.4 64.9 %all-to-all-start = ((bf16[8,128,256]{2,1,0:T(8,128)(2,1)}), bf16[8,128,256]{2,1,0:T(8,128)(2,1)S(1)}, u32[]{:S(2)}, u32[]{:S(2)}) async-start(bf16[8,128,256]{2,1,0:T(8,128)(2,1)} %broadcast_select_fusion), calls=%async_computation | async-start | bytes 1048576 | tf_op jit(solution)/shard_map/all_to_all | solution.py:534
  68.2 0.8 copy-start.4
  157.8 5.6 %copy-start.8 = (s32[32]{0:T(128)S(1)}, s32[32]{0:T(128)}, u32[]{:S(2)}) copy-start(s32[32]{0:T(128)} %param.32) | copy-start | bytes 388
  157.8 39.6 %all-to-all-start.1 = ((bf16[16,40,2048]{2,1,0:T(8,128)(2,1)}), bf16[16,40,2048]{2,1,0:T(8,128)(2,1)S(1)}, u32[]{:S(2)}, u32[]{:S(2)}) async-start(bf16[16,40,2048]{2,1,0:T(8,128)(2,1)} %bitcast.12), calls=%async_computation.1 | async-start | bytes 5242880 | tf_op jit(solution)/shard_map/all_to_all | solution.py:582
  197.4 27.9 %all-to-all-start.3 = ((bf16[16,8,2048]{2,1,0:T(8,128)(2,1)}), bf16[16,8,2048]{2,1,0:T(8,128)(2,1)S(1)}, u32[]{:S(2)}, u32[]{:S(2)}) async-start(bf16[16,8,2048]{2,1,0:T(8,128)(2,1)} %select_select_fusion), calls=%async_computation.3 | async-start | bytes 1048576 | tf_op jit(solution)/shard_map/all_to_all | solution.py:551
  225.2 7.8 %copy-start.7 = (f32[128,2]{0,1:T(2,128)S(1)}, f32[128,2]{0,1:T(2,128)}, u32[]{:S(2)}) copy-start(f32[128,2]{0,1:T(2,128)} %param.30) | copy-start | bytes 3076
  225.2 7.9 %copy-start.6 = (s32[1,4]{1,0:T(1,128)S(1)}, s32[1,4]{1,0:T(1,128)}, u32[]{:S(2)}) copy-start(s32[1,4]{1,0:T(1,128)} %param.24) | copy-start | bytes 52
  225.3 38.6 %all-to-all-start.2 = ((bf16[16,40,2048]{2,1,0:T(8,128)(2,1)}), bf16[16,40,2048]{2,1,0:T(8,128)(2,1)S(1)}, u32[]{:S(2)}, u32[]{:S(2)}) async-start(bf16[16,40,2048]{2,1,0:T(8,128)(2,1)} %fusion.4), calls=%async_computation.2 | async-start | bytes 5242880 | tf_op jit(solution)/shard_map/all_to_all | solution.py:589
  263.8 1.7 copy-start.2
  265.5 20.3 %all-to-all-start.4 = ((bf16[16,8,2048]{2,1,0:T(8,128)(2,1)}), bf16[16,8,2048]{2,1,0:T(8,128)(2,1)}, u32[]{:S(2)}, u32[]{:S(2)}) async-start(bf16[16,8,2048]{2,1,0:T(8,128)(2,1)} %broadcast_in_dim.132), calls=%async_computation.4 | async-start | bytes 1048576 | tf_op jit(solution)/shard_map/all_to_all | solution.py:554
  278.0 10.9 %copy-start.1 = (bf16[4,2,16,2048]{3,2,1,0:T(8,128)(2,1)S(1)}, bf16[4,2,16,2048]{3,2,1,0:T(8,128)(2,1)}, u32[]{:S(2)}) copy-start(bf16[4,2,16,2048]{3,2,1,0:T(8,128)(2,1)} %param.31) | copy-start | bytes 1572868
  280.6 5.2 %copy-start.3 = (bf16[128,2048]{1,0:T(8,128)(2,1)S(1)}, bf16[128,2048]{1,0:T(8,128)(2,1)}, u32[]{:S(2)}) copy-start(bf16[128,2048]{1,0:T(8,128)(2,1)} %get-tuple-element.14) | copy-start | bytes 1572868

commit v2 on v1

--- a/solution.py
+++ b/solution.py
@@ -53,6 +53,25 @@
     return barrier
 
 
+def meet_all(axis, here, count):
+    barrier = pltpu.get_barrier_semaphore()
+    for step in range(1, count):
+        other = lax.rem(here + step, count)
+        pl.semaphore_signal(barrier, inc=1, device_id={axis: other}, device_id_type=MESH)
+    return barrier
+
+
+def to_peer(axis, other, src, dst, send_sem, recv_sem):
+    return pltpu.make_async_remote_copy(
+        src_ref=src,
+        dst_ref=dst,
+        send_sem=send_sem,
+        recv_sem=recv_sem,
+        device_id={axis: other},
+        device_id_type=MESH,
+    )
+
+
 class Sender:
     def __init__(self, y, z, sems):
         self.y, self.z, self.sems, self.sent = y, z, sems, []
@@ -96,12 +115,16 @@
 
 
 def project_kernel(
-    lens, tok, gain, wq, wkv, freq, ids, q_out, k_out, v_out, held, w, acc, idt, ssem, rsem
+    lens, dest, wanted, tok, gain, wq, wkv, freq, ids, pool, adapters,
+    q_out, k_out, v_out, pages, factors,
+    held, w, acc, idt, leaving, parts_out, parts_in, ssem, rsem, page_ssem, page_sem, part_ssem, part_sem,
 ):
     me, y, z = place()
-    barrier = meet_neighbours(y, z)
+    group = lax.axis_index("req")
+    meet_all("exp", me, 16)
+    barrier = meet_all("req", group, 8)
     held[me] = rms_scale(tok[...], gain[0:1]).reshape(4, 32, -1)
-    pl.semaphore_wait(barrier, 4)
+    pl.semaphore_wait(barrier, 22)
     link = Sender(y, z, ssem)
 
     def send(s, piece, axis, step):
@@ -116,6 +139,52 @@
             for p in (0, 1):
                 for step in (1, 3):
                     send(me, 2 * half + p, (half + second) % 2, step)
+
+    def page_for(other):
+        block = pool[0]
+        for p in range(1, 4):
+            target = dest[group * 4 + p]
+            block = jnp.where((target >= other * 4) & (target < other * 4 + 4), pool[p], block)
+        return block
+
+    def part_for(other):
+        named = wanted[group * 4 + lax.div(other, 4)]
+        block = jnp.zeros(parts_in.shape[1:], BF16)
+        for a in range(4):
+            block = jnp.where(named == me * 4 + a, adapters[a, lax.rem(other, 4)], block)
+        return block
+
+    def page_step(step, carry):
+        other = lax.rem(group + step, 8)
+        leaving[step] = page_for(other)
+        return carry
+
+    def part_step(step, carry):
+        other = lax.rem(me + step, 16)
+        parts_out[step] = part_for(other)
+        return carry
+
+    lax.fori_loop(1, 8, page_step, 0)
+    lax.fori_loop(1, 16, part_step, 0)
+    pages[group] = page_for(group)
+    parts_in[0] = part_for(me)
+    others = []
+    for step in range(1, 8):
+        others.append(
+            to_peer(
+                "req", lax.rem(group + step, 8), leaving.at[step], pages.at[group],
+                page_ssem.at[step], page_sem.at[step],
+            )
+        )
+    for step in range(1, 16):
+        others.append(
+            to_peer(
+                "exp", lax.rem(me + step, 16), parts_out.at[step], parts_in.at[step],
+                part_ssem.at[step], part_sem.at[step],
+            )
+        )
+    for copy in others:
+        copy.start()
 
     rows256 = lax.broadcasted_iota(I32, (256, 256), 0)
     cols256 = lax.broadcasted_iota(I32, (256, 256), 1)
@@ -227,10 +296,16 @@
         return carry
 
     lax.fori_loop(0, 2, far_step, 0)
+    for copy in others:
+        copy.wait()
+    total = parts_in[0].astype(F32)
+    for step in range(1, 16):
+        total = total + parts_in[step].astype(F32)
+    factors[...] = total.astype(BF16)
     link.finish()
 
 
-def project(tokens, norm_gains, wq, wkv, lens, ids):
+def project(tokens, norm_gains, wq, wkv, lens, ids, dest, wanted, pool, adapters):
     rows = tokens.shape[0] * 16
     width = tokens.shape[1]
     lanes = np.arange(HD) % (HD // 2)
@@ -242,100 +317,109 @@
             jax.ShapeDtypeStruct((rows, 2 * HD), BF16),
             jax.ShapeDtypeStruct((rows, HD), BF16),
             jax.ShapeDtypeStruct((rows, HD), BF16),
+            jax.ShapeDtypeStruct((8,) + pool.shape[1:], BF16),
+            jax.ShapeDtypeStruct((8, width), BF16),
         ),
-        in_specs=[pl.BlockSpec(memory_space=pltpu.SMEM)] + [vmem] * 6,
-        out_specs=(vmem, vmem, vmem),
+        in_specs=[pl.BlockSpec(memory_space=pltpu.SMEM)] * 3 + [vmem] * 8,
+        out_specs=(vmem,) * 5,
         scratch_shapes=[
             pltpu.VMEM((16, 4, 32, width), BF16),
             pltpu.VMEM((width, 6 * HD), BF16),
             pltpu.VMEM((256, 6 * HD), F32),
             pltpu.VMEM((rows, 8), F32),
+            pltpu.VMEM((8,) + pool.shape[1:], BF16),
+            pltpu.VMEM((16, 8, width), BF16),
+            pltpu.VMEM((16, 8, width), BF16),
             pltpu.SemaphoreType.DMA((60,)),
             pltpu.SemaphoreType.DMA((16, 4)),
+            pltpu.SemaphoreType.DMA((8,)),
+            pltpu.SemaphoreType.DMA((8,)),
+            pltpu.SemaphoreType.DMA((16,)),
+            pltpu.SemaphoreType.DMA((16,)),
         ],
         compiler_params=pltpu.CompilerParams(collective_id=0, has_side_effects=True),
         name="gather_project",
-    )(lens, tokens, norm_gains, wq, wkv, jnp.asarray(freq), ids)
-
-
-def attend_kernel(lens, sender, q, k, v, pages, ids, gates, out, acc):
-    block = pl.program_id(0)
+    )(lens, dest, wanted, tokens, norm_gains, wq, wkv, jnp.asarray(freq), ids, pool, adapters)
+
+
+def attend_kernel(lens, dest, group, q, k, v, pages, ids, gates, out, acc):
     ends = ends_of(lens)
-    first = block * 128
-    last = first + 127
-    scale = 1.0 / math.sqrt(HD)
-    queries = jnp.concatenate([q[:, 0:HD], q[:, HD : 2 * HD]], axis=0)
-    rows = lax.broadcasted_iota(I32, (128, 1), 0) + first
-    rows = jnp.concatenate([rows, rows], axis=0)
-    begin = start_of(rows, ends)
-    low, high, low_start = 0, 0, 0
-    for end in ends[:3]:
-        low = low + (first >= end).astype(I32)
-        high = high + (last >= end).astype(I32)
-        low_start = jnp.where(first >= end, end, low_start)
-    acc[...] = jnp.zeros_like(acc)
-
-    def fold(state, keys, values, visible):
-        top, total = state
-        scores = lax.dot_general(
-            queries, keys, (((1,), (1,)), ((), ())), preferred_element_type=F32
-        )
-        scores = jnp.where(visible, scores * scale, -1e30)
-        peak = jnp.maximum(top, jnp.max(scores, axis=-1, keepdims=True))
-        kept = jnp.exp(top - peak)
-        raised = jnp.exp(scores - peak)
-        acc[...] = acc[...] * kept + jnp.dot(
-            raised.astype(BF16), values, preferred_element_type=F32
-        )
-        return peak, total * kept + jnp.sum(raised, axis=-1, keepdims=True)
-
-    def cached_step(r, state):
-        begins = jnp.where(r == 0, 0, jnp.where(r == 1, ends[0], jnp.where(r == 2, ends[1], ends[2])))
-        came = sender[r]
-        page = pages[came]
-        mine = jnp.broadcast_to(begin == begins, (256, CACHE))
-        return fold(state, page[:, 0:HD], page[:, HD : 2 * HD], mine)
-
-    def key_step(b, state):
-        at = pl.ds(pl.multiple_of(b * 256, 256), 256)
-        cols = lax.broadcasted_iota(I32, (256, 256), 1) + b * 256
-        return fold(state, k[at, :], v[at, :], (cols >= begin) & (cols <= rows))
-
-    state = (jnp.full((256, 1), -1e30, F32), jnp.zeros((256, 1), F32))
-    state = lax.fori_loop(low, high + 1, cached_step, state)
-    state = lax.fori_loop(lax.div(low_start, 256), lax.div(last, 256) + 1, key_step, state)
-    heads = (acc[...] / state[1]).astype(BF16).astype(F32)
-    named = jnp.concatenate([ids[...], jnp.zeros((6, 128), I32)], axis=0).astype(F32).T
-    weight = jnp.concatenate([gates[...], jnp.zeros((6, 128), F32)], axis=0).T
-    for e in range(AEXP):
-        mixed = jnp.zeros((128, HD), F32)
-        for j in (0, 1):
-            part = heads[j * 128 : (j + 1) * 128] * weight[:, j : j + 1]
-            mixed = mixed + jnp.where(named[:, j : j + 1] == float(e), part, 0.0)
-        out[:, e * HD : (e + 1) * HD] = mixed.astype(BF16)
-
-
-def attend(q, k, v, pages, lens, sender, ids, gates):
+    rate = math.log2(math.e) / math.sqrt(HD)
+    lane = lax.rem(lax.broadcasted_iota(I32, (1, 256), 1), 128)
+
+    def block_step(block, carry):
+        first = block * 128
+        last = first + 127
+        here = pl.ds(pl.multiple_of(first, 128), 128)
+        queries = jnp.concatenate([q[here, 0:HD], q[here, HD : 2 * HD]], axis=0)
+        rows = lane + first
+        begin = start_of(rows, ends)
+        low, high, low_start = 0, 0, 0
+        for end in ends[:3]:
+            low = low + (first >= end).astype(I32)
+            high = high + (last >= end).astype(I32)
+            low_start = jnp.where(first >= end, end, low_start)
+        acc[...] = jnp.zeros_like(acc)
+
+        def fold(state, keys, values, visible):
+            top, total = state
+            scores = lax.dot_general(
+                keys, queries, (((1,), (1,)), ((), ())), preferred_element_type=F32
+            )
+            scores = jnp.where(visible, scores, -1e30)
+            peak = jnp.maximum(top, jnp.max(scores, axis=0, keepdims=True))
+            kept = jnp.exp2((top - peak) * rate)
+            raised = jnp.exp2((scores - peak) * rate)
+            acc[...] = acc[...] * kept + lax.dot_general(
+                values, raised.astype(BF16), (((0,), (0,)), ((), ())), preferred_element_type=F32
+            )
+            return peak, total * kept + jnp.sum(raised, axis=0, keepdims=True)
+
+        def cached_step(r, state):
+            begins = jnp.where(
+                r == 0, 0, jnp.where(r == 1, ends[0], jnp.where(r == 2, ends[1], ends[2]))
+            )
+            came = 0
+            for g in range(8):
+                came = came + g * (dest[g * 4 + r] == group[0] * 4 + r).astype(I32)
+            page = pages[came]
+            mine = jnp.broadcast_to(begin == begins, (CACHE, 256))
+            return fold(state, page[:, 0:HD], page[:, HD : 2 * HD], mine)
+
+        def key_step(b, state):
+            at = pl.ds(pl.multiple_of(b * 256, 256), 256)
+            cols = lax.broadcasted_iota(I32, (256, 256), 0) + b * 256
+            return fold(state, k[at, :], v[at, :], (cols >= begin) & (cols <= rows))
+
+        state = (jnp.full((1, 256), -1e30, F32), jnp.zeros((1, 256), F32))
+        state = lax.fori_loop(low, high + 1, cached_step, state)
+        state = lax.fori_loop(lax.div(low_start, 256), lax.div(last, 256) + 1, key_step, state)
+        heads = (acc[...] / state[1]).astype(BF16).astype(F32)
+        named = jnp.concatenate([ids[:, here], jnp.zeros((6, 128), I32)], axis=0).astype(F32).T
+        weight = jnp.concatenate([gates[:, here], jnp.zeros((6, 128), F32)], axis=0).T
+        parts = [heads[:, j * 128 : (j + 1) * 128].T * weight[:, j : j + 1] for j in (0, 1)]
+        for e in range(AEXP):
+            mixed = jnp.zeros((128, HD), F32)
+            for j in (0, 1):
+                mixed = mixed + jnp.where(named[:, j : j + 1] == float(e), parts[j], 0.0)
+            out[here, e * HD : (e + 1) * HD] = mixed.astype(BF16)
+        return carry
+
+    lax.fori_loop(0, q.shape[0] // 128, block_step, 0)
+
+
+def attend(q, k, v, pages, lens, dest, group, ids, gates):
     rows = q.shape[0]
     smem = pl.BlockSpec(memory_space=pltpu.SMEM)
+    vmem = pl.BlockSpec(memory_space=pltpu.VMEM)
     return pl.pallas_call(
         attend_kernel,
         out_shape=jax.ShapeDtypeStruct((rows, AEXP * HD), BF16),
-        grid=(rows // 128,),
-        in_specs=[
-            smem,
-            smem,
-            pl.BlockSpec((128, 2 * HD), lambda i: (i, 0)),
-            pl.BlockSpec((rows, HD), lambda i: (0, 0)),
-            pl.BlockSpec((rows, HD), lambda i: (0, 0)),
-            pl.BlockSpec(pages.shape, lambda i: (0, 0, 0)),
-            pl.BlockSpec((2, 128), lambda i: (0, i)),
-            pl.BlockSpec((2, 128), lambda i: (0, i)),
-        ],
-        out_specs=pl.BlockSpec((128, AEXP * HD), lambda i: (i, 0)),
-        scratch_shapes=[pltpu.VMEM((256, HD), F32)],
+        in_specs=[smem] * 3 + [vmem] * 6,
+        out_specs=vmem,
+        scratch_shapes=[pltpu.VMEM((HD, 256), F32)],
         name="attend_mix",
-    )(lens, sender, q, k, v, pages, ids, gates)
+    )(lens, dest, group, q, k, v, pages, ids, gates)
 
 
 ORDER = (2, 1, 3, 0)
@@ -492,6 +576,169 @@
     )(mixed, w_out, tokens, norm_gains)
 
 
+def expert_kernel(
+    lens, hidden, hnorm, w_in, w_down, ids, gates, factors, out,
+    packed, rx, back, ret, raw, w, wd, both, placed, table,
+    wsem, dsem, ssem, rsem, bsem, esem, fsem, gsem,
+):
+    me = lax.axis_index("exp")
+    width = hidden.shape[1]
+    hidden_units = w_down.shape[0]
+    barrier = meet_all("exp", me, 16)
+    down = pltpu.make_async_copy(w_down, wd, dsem)
+    down.start()
+
+    def fetch(c):
+        return pltpu.make_async_copy(
+            w_in.at[pl.ds(c * 512, 512)], raw.at[lax.rem(c, 2)], wsem.at[lax.rem(c, 2)]
+        )
+
+    fetch(0).start()
+    expert = lax.broadcasted_iota(I32, (8, 128), 0)
+    hits = [ids[j : j + 1, :] == expert for j in (0, 1)]
+    hit = (hits[0] | hits[1]).astype(F32)
+    gate = jnp.where(hits[0], gates[0:1, :], 0.0) + jnp.where(hits[1], gates[1:2, :], 0.0)
+    before = lax.broadcasted_iota(I32, (128, 128), 0) < lax.broadcasted_iota(I32, (128, 128), 1)
+    rank = jnp.dot(hit.astype(BF16), before.astype(BF16), preferred_element_type=F32)
+    slot = lax.broadcasted_iota(I32, (CAP, 128), 0).astype(F32)
+    for e in range(EXPERTS):
+        placed[e] = jnp.where((rank[e : e + 1] == slot) & (hit[e : e + 1] > 0.0), 1.0, 0.0)
+    choice = placed[...].reshape(EXPERTS * CAP, 128).astype(BF16)
+    packed[...] = (
+        jnp.dot(choice, hnorm[...], preferred_element_type=F32).astype(BF16).reshape(packed.shape)
+    )
+    pl.semaphore_wait(barrier, 15)
+    copies = []
+    for step in range(1, 16):
+        other = lax.rem(me + step, 16)
+        copy = to_peer(
+            "exp", other, packed.at[lax.div(other, 2)], rx.at[step], ssem.at[step], rsem.at[step]
+        )
+        copy.start()
+        copies.append(copy)
+    rx[0] = packed[lax.div(me, 2)]
+
+    rows256 = lax.broadcasted_iota(I32, (256, 256), 0)
+    cols256 = lax.broadcasted_iota(I32, (256, 256), 1)
+    by2 = (cols256 == lax.rem(rows256, 128) * 2 + lax.div(rows256, 128)).astype(BF16)
+
+    def split_step(c, carry):
+        @pl.when(c + 1 < 8)
+        def _():
+            fetch(c + 1).start()
+
+        fetch(c).wait()
+        for b in (0, 1):
+            part = jnp.dot(
+                by2, raw[lax.rem(c, 2), b * 256 : (b + 1) * 256, :], preferred_element_type=F32
+            ).astype(BF16)
+            at = pl.ds(pl.multiple_of(c * 256 + b * 128, 128), 128)
+            w[at, 0:hidden_units] = part[0:128]
+            w[at, hidden_units : 2 * hidden_units] = part[128:256]
+        return carry
+
+    lax.fori_loop(0, 8, split_step, 0)
+    down.wait()
+    shares = []
+    for part in (0, 1):
+        for step in range(8 * part, 8 * part + 8):
+            if step:
+                copies[step - 1].wait_recv()
+        if part == 1:
+            for step in range(1, 16):
+                copy = to_peer(
+                    "exp", lax.rem(me + step, 16), factors, table.at[me], fsem.at[step], gsem.at[step]
+                )
+                copy.start()
+                shares.append(copy)
+        rows = rx[8 * part : 8 * part + 8].reshape(8 * CAP, width)
+        both[...] = jnp.dot(rows, w[...], preferred_element_type=F32)
+        gated = both[:, 0:hidden_units]
+        inner = (gated / (1.0 + jnp.exp(-gated)) * both[:, hidden_units : 2 * hidden_units]).astype(BF16)
+        back[8 * part : 8 * part + 8] = (
+            jnp.dot(inner, wd[...], preferred_element_type=F32).astype(BF16).reshape(8, CAP, width)
+        )
+        for step in range(8 * part, 8 * part + 8):
+            if step:
+                copy = to_peer(
+                    "exp", lax.rem(me + 16 - step, 16), back.at[step], ret.at[me],
+                    bsem.at[step], esem.at[step],
+                )
+                copy.start()
+                copies.append(copy)
+            else:
+                ret[me] = back[0]
+    table[me] = factors[...]
+    for copy in shares:
+        copy.wait()
+    rows = table[...].reshape(16 * 8, width)
+    lowrank = lax.dot_general(
+        hnorm[...], rows, (((1,), (1,)), ((), ())), preferred_element_type=F32
+    )
+    tokens = lax.broadcasted_iota(I32, (128, 1), 0) + me * 128
+    ends = ends_of(lens)
+    segment = jnp.zeros_like(tokens)
+    for end in ends[:3]:
+        segment = segment + (tokens >= end).astype(I32)
+    lane = lax.broadcasted_iota(I32, (128, 128), 1)
+    mine = (lax.div(lane, 32) == segment) & (lax.rem(lane, 32) < 16)
+    lowrank = pltpu.roll(jnp.where(mine, lowrank, 0.0), 16, 1).astype(BF16)
+    delta = jnp.dot(lowrank, rows, preferred_element_type=F32)
+    total = hidden[...].astype(F32) + delta
+    for step in range(1, 16):
+        copies[14 + step].wait_recv()
+    weight = jnp.concatenate(
+        [placed[e // 2] * gate[e // 2 : e // 2 + 1] for e in range(16)], axis=0
+    )
+    high = weight.astype(BF16)
+    low = (weight - high.astype(F32)).astype(BF16)
+    came = ret[...].reshape(16 * CAP, width)
+    for factor in (high, low):
+        total = total + lax.dot_general(
+            factor, came, (((0,), (0,)), ((), ())), preferred_element_type=F32
+        )
+    out[...] = total.astype(BF16)
+    for copy in copies:
+        copy.wait_send()
+
+
+def experts(hidden, hnorm, w_in, w_down, ids, gates, factors, lens):
+    rows, width = hidden.shape
+    units = w_down.shape[0]
+    smem = pl.BlockSpec(memory_space=pltpu.SMEM)
+    vmem = pl.BlockSpec(memory_space=pltpu.VMEM)
+    hbm = pl.BlockSpec(memory_space=pl.ANY)
+    dma = pltpu.SemaphoreType.DMA
+    return pl.pallas_call(
+        expert_kernel,
+        out_shape=jax.ShapeDtypeStruct((rows, width), BF16),
+        in_specs=[smem, vmem, vmem, hbm, hbm, vmem, vmem, vmem],
+        out_specs=vmem,
+        scratch_shapes=[
+            pltpu.VMEM((EXPERTS, CAP, width), BF16),
+            pltpu.VMEM((16, CAP, width), BF16),
+            pltpu.VMEM((16, CAP, width), BF16),
+            pltpu.VMEM((16, CAP, width), BF16),
+            pltpu.VMEM((2, 512, units), BF16),
+            pltpu.VMEM((width, 2 * units), BF16),
+            pltpu.VMEM((units, width), BF16),
+            pltpu.VMEM((8 * CAP, 2 * units), F32),
+            pltpu.VMEM((EXPERTS, CAP, 128), F32),
+            pltpu.VMEM((16, 8, width), BF16),
+            dma((2,)),
+            dma,
+            dma((16,)),
+            dma((16,)),
+            dma((16,)),
+            dma((16,)),
+            dma((16,)),
+            dma((16,)),
+        ],
+        compiler_params=pltpu.CompilerParams(collective_id=2, has_side_effects=True),
+        name="expert_exchange",
+    )(lens, hidden, hnorm, w_in, w_down, ids, gates, factors)
+
+
 def on_device(
     tokens,
     norm_gains,
@@ -510,97 +757,34 @@
     adapters,
     req_adapter,
 ):
-    groups = lax.axis_size("req")
-    columns = lax.axis_size("exp")
-    group_index = lax.axis_index("req")
-    column_index = lax.axis_index("exp")
-    tok_rows, width = tokens.shape
-    slot_count = page_pool.shape[0]
-    group_numbers = jnp.arange(groups, dtype=I32)
+    width = tokens.shape[1]
     lens = prompt_lens.reshape(-1)
-
-    own_target = (
-        lax.dynamic_slice_in_dim(page_dest, group_index * slot_count, slot_count) // slot_count
-    )
-    slot_for = jnp.sum(
-        jnp.where(
-            own_target[None, :] == group_numbers[:, None],
-            jnp.arange(slot_count, dtype=I32)[None, :],
-            0,
-        ),
-        axis=1,
-    )
-    outgoing = jnp.take(page_pool.reshape(slot_count, CACHE, 2 * HD), slot_for, axis=0)
-    pages = lax.all_to_all(outgoing, "req", split_axis=0, concat_axis=0, tiled=True)
-    pool_slots = jnp.arange(page_dest.shape[0], dtype=I32)
-    wanted = group_index * slot_count + jnp.arange(slot_count, dtype=I32)
-    sender = (
-        jnp.sum(jnp.where(page_dest[None, :] == wanted[:, None], pool_slots[None, :], 0), axis=1)
-        // slot_count
-    )
-
-    wanted_ids = lax.dynamic_slice_in_dim(req_adapter, group_index * slot_count, slot_count)
-    local_ids = wanted_ids - column_index * adapters.shape[0]
-    held_here = (local_ids >= 0) & (local_ids < adapters.shape[0])
-    share = jnp.where(
-        held_here[:, None, None, None],
-        jnp.take(adapters, jnp.clip(local_ids, 0, adapters.shape[0] - 1), axis=0),
-        jnp.zeros((), BF16),
-    )
-    share = share.reshape(columns, -1, width)
-    pieces = lax.all_to_all(share, "exp", split_axis=0, concat_axis=0, tiled=True)
-    whole = jnp.sum(pieces.astype(F32), axis=0).astype(BF16)
-    spread = jnp.broadcast_to(whole[None], share.shape)
-    group_factors = lax.all_to_all(spread, "exp", split_axis=0, concat_axis=0, tiled=True)
-    group_factors = group_factors.reshape(slot_count, *adapters.shape[1:])
-
+    group = lax.axis_index("req").reshape(1)
     ids = att_ids.T
-    q, k, v = project(
+    q, k, v, pages, factors = project(
         tokens,
         norm_gains,
         w_query.reshape(width * AEXP, HD),
         w_keyval.reshape(width * 2, HD),
         lens,
         ids,
+        page_dest,
+        req_adapter,
+        page_pool.reshape(page_pool.shape[0], CACHE, 2 * HD),
+        adapters.reshape(adapters.shape[0], 4, 8, width),
     )
-    mixed = attend(q, k, v, pages, lens, sender, ids, att_gates.T)
-    hidden_state, hnorm = reduce_out(mixed, w_out.reshape(-1, width), tokens, norm_gains)
-
-    expert_flat = moe_ids.reshape(-1)
-    expert_hits = (expert_flat[:, None] == jnp.arange(EXPERTS, dtype=I32)[None, :]).astype(I32)
-    earlier = jnp.cumsum(expert_hits, axis=0) - expert_hits
-    route_slot = jnp.sum(earlier * expert_hits, axis=1) + expert_flat * CAP
-    table_size = EXPERTS * CAP
-    placing = (jnp.arange(table_size, dtype=I32)[:, None] == route_slot[None, :]).reshape(
-        table_size, tok_rows, 2
+    mixed = attend(q, k, v, pages, lens, page_dest, group, ids, att_gates.T)
+    hidden, hnorm = reduce_out(mixed, w_out.reshape(-1, width), tokens, norm_gains)
+    return experts(
+        hidden,
+        hnorm,
+        w_in.reshape(width * 2, -1),
+        w_down,
+        moe_ids.T,
+        moe_gates.T,
+        factors,
+        lens,
     )
-    placing = jnp.any(placing, axis=2).astype(BF16)
-    packed = jnp.dot(placing, hnorm, preferred_element_type=F32).astype(BF16)
-    packed = packed.reshape(EXPERTS, CAP, width)
-    copies = columns // EXPERTS
-    spread_rows = jnp.repeat(packed, copies, axis=0)
-    arrived = lax.all_to_all(spread_rows, "exp", split_axis=0, concat_axis=0, tiled=True)
-    flat_rows = arrived.reshape(-1, width)
-    gate_up = jnp.einsum("nd,dkf->nkf", flat_rows, w_in, preferred_element_type=F32)
-    inner_act = (jax.nn.silu(gate_up[:, 0]) * gate_up[:, 1]).astype(BF16)
-    partial_out = jnp.dot(inner_act, w_down, preferred_element_type=F32).reshape(
-        columns, CAP, width
-    )
-    returned = lax.all_to_all(
-        partial_out.astype(BF16), "exp", split_axis=0, concat_axis=0, tiled=True
-    ).astype(F32)
-    summed = jnp.sum(returned.reshape(EXPERTS, copies, CAP, width), axis=1).reshape(
-        table_size, width
-    )
-    routed_rows = jnp.take(summed, route_slot, axis=0).reshape(tok_rows, 2, width)
-    expert_out = jnp.sum(routed_rows * moe_gates[:, :, None], axis=1)
-    own_rows = column_index * tok_rows + jnp.arange(tok_rows, dtype=I32)
-    own_segment = jnp.sum((own_rows[:, None] >= jnp.cumsum(lens)[None, :]).astype(I32), axis=1)
-    lowrank = jnp.einsum("td,qrd->tqr", hnorm, group_factors[:, 0], preferred_element_type=F32)
-    member = own_segment[:, None] == jnp.arange(slot_count, dtype=I32)[None, :]
-    lowrank = jnp.where(member[:, :, None], lowrank, 0.0).astype(BF16)
-    delta = jnp.einsum("tqr,qrd->td", lowrank, group_factors[:, 1], preferred_element_type=F32)
-    return (hidden_state.astype(F32) + expert_out + delta).astype(BF16)
 
 
 def solution(mesh):

time: 290 us -> 275 us (0.948)
  Pallas kernels: 143 us -> 248 us
  waiting for transfers between devices: 60.5 us -> 0 us
  starting transfers between devices: 32.4 us -> 0 us
  matrix products: 24.8 us -> 0 us
  other arithmetic: 13.5 us -> 0 us
  local copies, waits for them, and re-layouts: 14.6 us -> 25.7 us
    pallas_call x0 -> x1, Pallas kernels: none -> 98.7 us  [experts(): pl.pallas_call(expert_kernel, out_shape=jax.ShapeDtypeStruct((rows, width...]
    all_to_all x5 -> x0, waiting for transfers between devices: 60.5 us -> none  [the longest x1 30.3 us: on_device(): lax.all_to_all(partial_out.astype(BF16), 'exp', split_axis=0, concat_axis...]
    all_to_all x5 -> x0, starting transfers between devices: 32.4 us -> none  [the longest x1 7.37 us: on_device(): lax.all_to_all(partial_out.astype(BF16), 'exp', split_axis=0, concat_axis...]
    dot_general x4 -> x0, matrix products: 24.8 us -> none  [the longest x1 11.7 us: on_device(): jnp.einsum('nd,dkf->nkf', flat_rows, w_in, preferred_element_type=F32)]
    reshape x0 -> x1, local copies, waits for them, and re-layouts: none -> 23.8 us  [on_device(): w_in.reshape(width * 2, -1)]
    reduce_sum x7 -> x0, other arithmetic: 8.28 us -> none  [the longest x1 5.17 us: on_device(): expert_out = jnp.sum(routed_rows * moe_gates[:, :, None], axis=1)]
    gather x4 -> x0, local copies, waits for them, and re-layouts: 8.16 us -> none  [the longest x2 5.26 us: on_device(): jnp.take(summed, route_slot, axis=0).reshape(tok_rows, 2, width)]
    pallas_call x1, Pallas kernels: 57.6 us -> 64.3 us  [project(): pl.pallas_call(project_kernel, out_shape=(jax.ShapeDtypeStruct((rows, 2 *...]
  transfers between devices with their start and end apart: 5 -> 0, of which waited for: 2 -> 0; matrix products, arithmetic and copies ran while one was open for 14% -> 0% of each run, Pallas kernels for 20% -> 0%
where the time goes in v2:
time: 275 us; the launch traced here: 274 us
  Pallas kernels  248 us (90%)
  local copies, waits for them, and re-layouts  25.7 us (9%)
    pallas_call x1, Pallas kernels, experts(): pl.pallas_call(expert_kernel, out_shape=jax.ShapeDtypeStruct((rows, width...  98.7 us
    pallas_call x1, Pallas kernels, project(): pl.pallas_call(project_kernel, out_shape=(jax.ShapeDtypeStruct((rows, 2 *...  64.3 us
    pallas_call x1, Pallas kernels, reduce_out(): pl.pallas_call(reduce_kernel, out_shape=(shape, shape), in_specs=[vmem] *...  51.4 us
    pallas_call x1, Pallas kernels, attend(): pl.pallas_call(attend_kernel, out_shape=jax.ShapeDtypeStruct((rows, AEXP...  33.9 us
    reshape x1, local copies, waits for them, and re-layouts, on_device(): w_in.reshape(width * 2, -1)  23.8 us

profile of v2, /device:TPU:14, one launch (start us, length us, event | category | flops | bytes accessed | tf_op | source)
XLA Modules:
  0.0 274.0 jit_solution(15438780748269562705)
XLA Ops:
  0.0 64.3 %gather_project.1 = (bf16[2048,256]{1,0:T(8,128)(2,1)}, bf16[2048,128]{1,0:T(8,128)(2,1)}, bf16[2048,128]{1,0:T(8,128)(2,1)}, bf16[8,128,256]{2,1,0:T(8,128)(2,1)}, bf16[8,2048]{1,0:T(8,128)(2,1)}) custom-call(s32[4]{0:T(128)} %bitcast.19, s32[32]{0:T(128)} %dest.3, s32[32]{0:T(128)} %wanted.1, bf16[128,2048]{1,0:T(8,128)(2,1)} %tok.3, f32[2,2048]{1,0:T(2,128)} %gain.3, ...), custom_call_target="tpu_custom_call" | custom-call | tf_op jit(solution)/shard_map/gather_project/pallas_call | solution.py:314
  64.3 33.9 %attend_mix.1.mixed = bf16[2048,512]{1,0:T(8,128)(2,1)} custom-call(s32[4]{0:T(128)} %bitcast.20, s32[32]{0:T(128)} %dest.3, s32[1]{0:T(128)} %bitcast.1.group, bf16[2048,256]{1,0:T(8,128)(2,1)} %get-tuple-element.12.q, bf16[2048,128]{1,0:T(8,128)(2,1)} %get-tuple-element.13.k, bf16[2048,128]{1,0:T(8,128)(2,1)} %get-tuple-element.14.v, ...), custom_call_target="tpu_custom_call" | custom-call | tf_op jit(solution)/shard_map/attend_mix/pallas_call | solution.py:415
  98.2 51.4 %project_reduce.1 = (bf16[128,2048]{1,0:T(8,128)(2,1)}, bf16[128,2048]{1,0:T(8,128)(2,1)}) custom-call(bf16[2048,512]{1,0:T(8,128)(2,1)} %attend_mix.1.mixed, bf16[512,2048]{1,0:T(8,128)(2,1)} %bitcast.12, bf16[128,2048]{1,0:T(8,128)(2,1)} %tok.3, f32[2,2048]{1,0:T(2,128)} %gain.3), custom_call_target="tpu_custom_call" | custom-call | tf_op jit(solution)/shard_map/project_reduce/pallas_call | solution.py:553
  149.6 23.8 %reshape.31.w_in = bf16[4096,1408]{1,0:T(8,128)(2,1)} reshape(bf16[2048,2,1408]{2,1,0:T(2,128)(2,1)} %param.27) | data formatting | bytes 23068672 | tf_op jit(solution)/shard_map/reshape | solution.py:781
  173.4 98.7 %expert_exchange.1 = bf16[128,2048]{1,0:T(8,128)(2,1)} custom-call(s32[4]{0:T(128)} %bitcast.21, bf16[128,2048]{1,0:T(8,128)(2,1)} %get-tuple-element.16.hidden, bf16[128,2048]{1,0:T(8,128)(2,1)} %get-tuple-element.17.hnorm, bf16[4096,1408]{1,0:T(8,128)(2,1)} %reshape.31.w_in, bf16[1408,2048]{1,0:T(8,128)(2,1)} %w_down.1, s32[2,128]{1,0:T(2,128)} %bitcast.22, ...), custom_call_target="tpu_custom_call" | custom-call | tf_op jit(solution)/shard_map/expert_exchange/pallas_call | solution.py:712
  272.1 1.9 copy.19

commit v3 on v2

--- a/solution.py
+++ b/solution.py
@@ -14,6 +14,7 @@
 CACHE = 128
 CAP = 40
 SIDE = 4
+RATE = math.log2(math.e) / math.sqrt(HD)
 MESH = pl.DeviceIdType.MESH
 F32, BF16, I32 = jnp.float32, jnp.bfloat16, jnp.int32
 
@@ -115,9 +116,9 @@
 
 
 def project_kernel(
-    lens, dest, wanted, tok, gain, wq, wkv, freq, ids, pool, adapters,
-    q_out, k_out, v_out, pages, factors,
-    held, w, acc, idt, leaving, parts_out, parts_in, ssem, rsem, page_ssem, page_sem, part_ssem, part_sem,
+    lens, dest, wanted, tok, gain, wq, wkv, freq, ids, gates, pool, adapters,
+    q_out, k_out, v_out, pages, factors, idt,
+    held, w, acc, waves, leaving, parts_out, parts_in, ssem, rsem, page_ssem, page_sem, part_ssem, part_sem,
 ):
     me, y, z = place()
     group = lax.axis_index("req")
@@ -140,6 +141,80 @@
                 for step in (1, 3):
                     send(me, 2 * half + p, (half + second) % 2, step)
 
+    rows256 = lax.broadcasted_iota(I32, (256, 256), 0)
+    cols256 = lax.broadcasted_iota(I32, (256, 256), 1)
+    by4 = (cols256 == lax.rem(rows256, 64) * 4 + lax.div(rows256, 64)).astype(BF16)
+    by2 = (cols256 == lax.rem(rows256, 128) * 2 + lax.div(rows256, 128)).astype(BF16)
+
+    def split4(b, carry):
+        part = jnp.dot(by4, wq[pl.ds(b * 256, 256), :], preferred_element_type=F32).astype(BF16)
+        for e in range(4):
+            w[pl.ds(b * 64, 64), e * HD : (e + 1) * HD] = part[e * 64 : (e + 1) * 64]
+        return carry
+
+    def split2(b, carry):
+        part = jnp.dot(by2, wkv[pl.ds(b * 256, 256), :], preferred_element_type=F32).astype(BF16)
+        for e in range(2):
+            w[pl.ds(b * 128, 128), (4 + e) * HD : (5 + e) * HD] = part[e * 128 : (e + 1) * 128]
+        return carry
+
+    lax.fori_loop(0, 32, split4, 0, unroll=2)
+
+    def turn_ids(b, carry):
+        at = pl.ds(pl.multiple_of(b * 128, 128), 128)
+        block = jnp.concatenate(
+            [ids[:, at].astype(F32), gates[:, at], jnp.zeros((4, 128), F32)], axis=0
+        )
+        idt[at, :] = block.T
+        rows = lax.broadcasted_iota(I32, (128, 1), 0) + b * 128
+        places = CACHE + rows - start_of(rows, ends)
+        waves[at, :] = jnp.cos(places.astype(F32) * freq[0:1] - freq[1:2])
+        return carry
+
+    ends = ends_of(lens)
+    lane = lax.broadcasted_iota(I32, (256, HD), 1)
+
+    def project(half, across):
+        shards = [a * (4 - 3 * half) + across * (1 + 3 * half) for a in range(4)]
+        lhs = jnp.concatenate(
+            [held[s, pl.ds(2 * half, 2)].reshape(64, -1) for s in shards], axis=0
+        )
+        acc[...] = jnp.dot(lhs, w[...], preferred_element_type=F32)
+        starts = [pl.multiple_of(s * 128 + half * 64, 64) for s in shards]
+        wave = jnp.concatenate([waves[pl.ds(at, 64), :] for at in starts], axis=0)
+        swapped = pltpu.roll(wave, HD // 2, 1)
+        cosine = jnp.where(lane < HD // 2, wave, swapped)
+        sine = jnp.where(lane < HD // 2, -swapped, wave)
+
+        def turn(v):
+            return (v * cosine + pltpu.roll(v, HD // 2, 1) * sine).astype(BF16)
+
+        named = jnp.concatenate([idt[pl.ds(at, 64), :] for at in starts], axis=0)
+        slots = []
+        for j in (0, 1):
+            pick = acc[:, 0:HD]
+            for e in range(1, 4):
+                pick = jnp.where(named[:, j : j + 1] == float(e), acc[:, e * HD : (e + 1) * HD], pick)
+            slots.append(turn(pick * RATE))
+        keys = turn(acc[:, 4 * HD : 5 * HD])
+        values = acc[:, 5 * HD : 6 * HD].astype(BF16)
+        for a in range(4):
+            at, piece = pl.ds(starts[a], 64), slice(a * 64, (a + 1) * 64)
+            q_out[at, 0:HD] = slots[0][piece]
+            q_out[at, HD : 2 * HD] = slots[1][piece]
+            k_out[at, :] = keys[piece]
+            v_out[at, :] = values[piece]
+
+    for half in (0, 1):
+        for first, piece, step in ((3, 0, 1), (1, 1, 3)):
+            s = shard_at(y, z, half, first, 0)
+            arrive(s, half)
+            send(s, 2 * half + piece, half, step)
+            for p in (0, 1):
+                for onward in (1, 3):
+                    send(s, 2 * half + p, 1 - half, onward)
+    lax.fori_loop(0, 16, split2, 0, unroll=2)
+    lax.fori_loop(0, 16, turn_ids, 0)
     def page_for(other):
         block = pool[0]
         for p in range(1, 4):
@@ -186,79 +261,6 @@
     for copy in others:
         copy.start()
 
-    rows256 = lax.broadcasted_iota(I32, (256, 256), 0)
-    cols256 = lax.broadcasted_iota(I32, (256, 256), 1)
-    by4 = (cols256 == lax.rem(rows256, 64) * 4 + lax.div(rows256, 64)).astype(BF16)
-    by2 = (cols256 == lax.rem(rows256, 128) * 2 + lax.div(rows256, 128)).astype(BF16)
-
-    def split4(b, carry):
-        part = jnp.dot(by4, wq[pl.ds(b * 256, 256), :], preferred_element_type=F32).astype(BF16)
-        for e in range(4):
-            w[pl.ds(b * 64, 64), e * HD : (e + 1) * HD] = part[e * 64 : (e + 1) * 64]
-        return carry
-
-    def split2(b, carry):
-        part = jnp.dot(by2, wkv[pl.ds(b * 256, 256), :], preferred_element_type=F32).astype(BF16)
-        for e in range(2):
-            w[pl.ds(b * 128, 128), (4 + e) * HD : (5 + e) * HD] = part[e * 128 : (e + 1) * 128]
-        return carry
-
-    lax.fori_loop(0, 32, split4, 0)
-    lax.fori_loop(0, 16, split2, 0)
-
-    def turn_ids(b, carry):
-        at = pl.ds(pl.multiple_of(b * 128, 128), 128)
-        block = jnp.concatenate([ids[:, at], jnp.zeros((6, 128), I32)], axis=0)
-        idt[at, :] = block.astype(F32).T
-        return carry
-
-    lax.fori_loop(0, 16, turn_ids, 0)
-    ends = ends_of(lens)
-    lane = lax.broadcasted_iota(I32, (256, HD), 1)
-
-    def project(half, across):
-        shards = [a * (4 - 3 * half) + across * (1 + 3 * half) for a in range(4)]
-        lhs = jnp.concatenate(
-            [held[s, pl.ds(2 * half, 2)].reshape(64, -1) for s in shards], axis=0
-        )
-        acc[...] = jnp.dot(lhs, w[...], preferred_element_type=F32)
-        starts = [pl.multiple_of(s * 128 + half * 64, 64) for s in shards]
-        rows = jnp.concatenate(
-            [lax.broadcasted_iota(I32, (64, 1), 0) + at for at in starts], axis=0
-        )
-        places = CACHE + rows - start_of(rows, ends)
-        angle = places.astype(F32) * freq[...]
-        cosine = jnp.cos(angle)
-        sine = jnp.sin(angle)
-        sine = jnp.where(lane < HD // 2, -sine, sine)
-
-        def turn(v):
-            return (v * cosine + pltpu.roll(v, HD // 2, 1) * sine).astype(BF16)
-
-        named = jnp.concatenate([idt[pl.ds(at, 64), :] for at in starts], axis=0)
-        slots = []
-        for j in (0, 1):
-            pick = acc[:, 0:HD]
-            for e in range(1, 4):
-                pick = jnp.where(named[:, j : j + 1] == float(e), acc[:, e * HD : (e + 1) * HD], pick)
-            slots.append(turn(pick))
-        keys = turn(acc[:, 4 * HD : 5 * HD])
-        values = acc[:, 5 * HD : 6 * HD].astype(BF16)
-        for a in range(4):
-            at, piece = pl.ds(starts[a], 64), slice(a * 64, (a + 1) * 64)
-            q_out[at, 0:HD] = slots[0][piece]
-            q_out[at, HD : 2 * HD] = slots[1][piece]
-            k_out[at, :] = keys[piece]
-            v_out[at, :] = values[piece]
-
-    for half in (0, 1):
-        for first, piece, step in ((3, 0, 1), (1, 1, 3)):
-            s = shard_at(y, z, half, first, 0)
-            arrive(s, half)
-            send(s, 2 * half + piece, half, step)
-            for p in (0, 1):
-                for onward in (1, 3):
-                    send(s, 2 * half + p, 1 - half, onward)
     for half in (0, 1):
         s = shard_at(y, z, half, 2, 0)
         arrive(s, half)
@@ -305,11 +307,13 @@
     link.finish()
 
 
-def project(tokens, norm_gains, wq, wkv, lens, ids, dest, wanted, pool, adapters):
+def project(tokens, norm_gains, wq, wkv, lens, ids, gates, dest, wanted, pool, adapters):
     rows = tokens.shape[0] * 16
     width = tokens.shape[1]
     lanes = np.arange(HD) % (HD // 2)
-    freq = np.power(10000.0, lanes * (-2.0 / HD)).astype(np.float32)[None, :]
+    freq = np.stack(
+        [np.power(10000.0, lanes * (-2.0 / HD)), (np.arange(HD) // (HD // 2)) * (np.pi / 2)]
+    ).astype(np.float32)
     vmem = pl.BlockSpec(memory_space=pltpu.VMEM)
     return pl.pallas_call(
         project_kernel,
@@ -319,14 +323,15 @@
             jax.ShapeDtypeStruct((rows, HD), BF16),
             jax.ShapeDtypeStruct((8,) + pool.shape[1:], BF16),
             jax.ShapeDtypeStruct((8, width), BF16),
+            jax.ShapeDtypeStruct((rows, 8), F32),
         ),
-        in_specs=[pl.BlockSpec(memory_space=pltpu.SMEM)] * 3 + [vmem] * 8,
-        out_specs=(vmem,) * 5,
+        in_specs=[pl.BlockSpec(memory_space=pltpu.SMEM)] * 3 + [vmem] * 9,
+        out_specs=(vmem,) * 6,
         scratch_shapes=[
             pltpu.VMEM((16, 4, 32, width), BF16),
             pltpu.VMEM((width, 6 * HD), BF16),
             pltpu.VMEM((256, 6 * HD), F32),
-            pltpu.VMEM((rows, 8), F32),
+            pltpu.VMEM((rows, HD), F32),
             pltpu.VMEM((8,) + pool.shape[1:], BF16),
             pltpu.VMEM((16, 8, width), BF16),
             pltpu.VMEM((16, 8, width), BF16),
@@ -339,13 +344,29 @@
         ],
         compiler_params=pltpu.CompilerParams(collective_id=0, has_side_effects=True),
         name="gather_project",
-    )(lens, dest, wanted, tokens, norm_gains, wq, wkv, jnp.asarray(freq), ids, pool, adapters)
-
-
-def attend_kernel(lens, dest, group, q, k, v, pages, ids, gates, out, acc):
+    )(lens, dest, wanted, tokens, norm_gains, wq, wkv, jnp.asarray(freq), ids, gates, pool, adapters)
+
+
+def attend_kernel(lens, dest, group, q, k, v, pages, out, acc, turned, page_turned):
     ends = ends_of(lens)
-    rate = math.log2(math.e) / math.sqrt(HD)
     lane = lax.rem(lax.broadcasted_iota(I32, (1, 256), 1), 128)
+    ones = jnp.ones((8, 128), BF16)
+
+    def turn_step(b, carry):
+        at = pl.ds(pl.multiple_of(b * 128, 128), 128)
+        turned[0:HD, at] = v[at, :].astype(F32).T.astype(BF16)
+        turned[HD : HD + 8, at] = ones
+        return carry
+
+    lax.fori_loop(0, v.shape[0] // 128, turn_step, 0)
+    came = []
+    for r in range(4):
+        at = 0
+        for g in range(8):
+            at = at + g * (dest[g * 4 + r] == group[0] * 4 + r).astype(I32)
+        came.append(at)
+        page_turned[r, 0:HD] = pages[at, :, HD : 2 * HD].astype(F32).T.astype(BF16)
+        page_turned[r, HD : HD + 8] = ones
 
     def block_step(block, carry):
         first = block * 128
@@ -354,79 +375,83 @@
         queries = jnp.concatenate([q[here, 0:HD], q[here, HD : 2 * HD]], axis=0)
         rows = lane + first
         begin = start_of(rows, ends)
-        low, high, low_start = 0, 0, 0
+        low, high, low_start, high_start = 0, 0, 0, 0
         for end in ends[:3]:
             low = low + (first >= end).astype(I32)
             high = high + (last >= end).astype(I32)
             low_start = jnp.where(first >= end, end, low_start)
+            high_start = jnp.where(last >= end, end, high_start)
         acc[...] = jnp.zeros_like(acc)
 
-        def fold(state, keys, values, visible):
-            top, total = state
+        def fold(top, keys, values, visible):
             scores = lax.dot_general(
                 keys, queries, (((1,), (1,)), ((), ())), preferred_element_type=F32
             )
-            scores = jnp.where(visible, scores, -1e30)
+            if visible is not None:
+                scores = jnp.where(visible, scores, -1e30)
             peak = jnp.maximum(top, jnp.max(scores, axis=0, keepdims=True))
-            kept = jnp.exp2((top - peak) * rate)
-            raised = jnp.exp2((scores - peak) * rate)
-            acc[...] = acc[...] * kept + lax.dot_general(
-                values, raised.astype(BF16), (((0,), (0,)), ((), ())), preferred_element_type=F32
-            )
-            return peak, total * kept + jnp.sum(raised, axis=0, keepdims=True)
-
-        def cached_step(r, state):
+            kept = jnp.exp2(top - peak)
+            raised = jnp.exp2(scores - peak).astype(BF16)
+            acc[...] = acc[...] * kept + jnp.dot(values, raised, preferred_element_type=F32)
+            return peak
+
+        def cached_step(r, top):
             begins = jnp.where(
                 r == 0, 0, jnp.where(r == 1, ends[0], jnp.where(r == 2, ends[1], ends[2]))
             )
-            came = 0
-            for g in range(8):
-                came = came + g * (dest[g * 4 + r] == group[0] * 4 + r).astype(I32)
-            page = pages[came]
+            page = jnp.where(
+                r == 0, came[0], jnp.where(r == 1, came[1], jnp.where(r == 2, came[2], came[3]))
+            )
             mine = jnp.broadcast_to(begin == begins, (CACHE, 256))
-            return fold(state, page[:, 0:HD], page[:, HD : 2 * HD], mine)
-
-        def key_step(b, state):
+            return fold(top, pages[page, :, 0:HD], page_turned[r], mine)
+
+        def masked_step(b, top):
             at = pl.ds(pl.multiple_of(b * 256, 256), 256)
             cols = lax.broadcasted_iota(I32, (256, 256), 0) + b * 256
-            return fold(state, k[at, :], v[at, :], (cols >= begin) & (cols <= rows))
-
-        state = (jnp.full((1, 256), -1e30, F32), jnp.zeros((1, 256), F32))
-        state = lax.fori_loop(low, high + 1, cached_step, state)
-        state = lax.fori_loop(lax.div(low_start, 256), lax.div(last, 256) + 1, key_step, state)
-        heads = (acc[...] / state[1]).astype(BF16).astype(F32)
-        named = jnp.concatenate([ids[:, here], jnp.zeros((6, 128), I32)], axis=0).astype(F32).T
-        weight = jnp.concatenate([gates[:, here], jnp.zeros((6, 128), F32)], axis=0).T
-        parts = [heads[:, j * 128 : (j + 1) * 128].T * weight[:, j : j + 1] for j in (0, 1)]
-        for e in range(AEXP):
-            mixed = jnp.zeros((128, HD), F32)
-            for j in (0, 1):
-                mixed = mixed + jnp.where(named[:, j : j + 1] == float(e), parts[j], 0.0)
-            out[here, e * HD : (e + 1) * HD] = mixed.astype(BF16)
+            return fold(top, k[at, :], turned[:, at], (cols >= begin) & (cols <= rows))
+
+        def plain_step(b, top):
+            at = pl.ds(pl.multiple_of(b * 256, 256), 256)
+            return fold(top, k[at, :], turned[:, at], None)
+
+        top = jnp.full((1, 256), -1e30, F32)
+        top = lax.fori_loop(low, high + 1, cached_step, top)
+        start, stop = lax.div(low_start, 256), lax.div(last, 256)
+        clear = jnp.minimum(jnp.maximum(lax.div(high_start + 255, 256), start), stop)
+        top = lax.fori_loop(start, clear, masked_step, top)
+        top = lax.fori_loop(clear, stop, plain_step, top)
+        top = masked_step(stop, top)
+        heads = acc[0:HD] / acc[HD : HD + 1]
+        out[here, 0:HD] = heads[:, 0:128].T.astype(BF16)
+        out[here, HD : 2 * HD] = heads[:, 128:256].T.astype(BF16)
         return carry
 
     lax.fori_loop(0, q.shape[0] // 128, block_step, 0)
 
 
-def attend(q, k, v, pages, lens, dest, group, ids, gates):
+def attend(q, k, v, pages, lens, dest, group):
     rows = q.shape[0]
     smem = pl.BlockSpec(memory_space=pltpu.SMEM)
     vmem = pl.BlockSpec(memory_space=pltpu.VMEM)
     return pl.pallas_call(
         attend_kernel,
-        out_shape=jax.ShapeDtypeStruct((rows, AEXP * HD), BF16),
-        in_specs=[smem] * 3 + [vmem] * 6,
+        out_shape=jax.ShapeDtypeStruct((rows, 2 * HD), BF16),
+        in_specs=[smem] * 3 + [vmem] * 4,
         out_specs=vmem,
-        scratch_shapes=[pltpu.VMEM((HD, 256), F32)],
-        name="attend_mix",
-    )(lens, dest, group, q, k, v, pages, ids, gates)
+        scratch_shapes=[
+            pltpu.VMEM((HD + 8, 256), F32),
+            pltpu.VMEM((HD + 8, rows), BF16),
+            pltpu.VMEM((4, HD + 8, CACHE), BF16),
+        ],
+        name="attend_heads",
+    )(lens, dest, group, q, k, v, pages)
 
 
 ORDER = (2, 1, 3, 0)
 
 
 def reduce_kernel(
-    mixed, w, tok, gain, hidden, hnorm, far, near, own, rx_far, rx_near, far2, near2, rx_far2, rx_near2,
+    heads, choice, w, tok, gain, hidden, hnorm, far, near, own, rx_far, rx_near, far2, near2, rx_far2, rx_near2,
     ssem, far_sem, near_sem, far2_sem, near2_sem,
 ):
     me, y, z = place()
@@ -439,8 +464,15 @@
         for offset in ORDER:
             two = lax.rem(z * (1 - half) + y * half + offset, SIDE)
             s = one * (4 - 3 * half) + two * (1 + 3 * half)
-            parts.append(mixed[pl.ds(pl.multiple_of(s * 128 + half * 64, 64), 64), :])
-        return jnp.dot(jnp.concatenate(parts, axis=0), w[...], preferred_element_type=F32)
+            parts.append(pl.ds(pl.multiple_of(s * 128 + half * 64, 64), 64))
+        rows = jnp.concatenate([heads[at, :] for at in parts], axis=0).astype(F32)
+        named = jnp.concatenate([choice[at, :] for at in parts], axis=0)
+        gated = [rows[:, j * HD : (j + 1) * HD] * named[:, 2 + j : 3 + j] for j in (0, 1)]
+        mixed = []
+        for e in range(AEXP):
+            both = [jnp.where(named[:, j : j + 1] == float(e), gated[j], 0.0) for j in (0, 1)]
+            mixed.append((both[0] + both[1]).astype(BF16))
+        return jnp.dot(jnp.concatenate(mixed, axis=1), w[...], preferred_element_type=F32)
 
     def far_step(half, carry):
         far[half] = partial(half, 2).astype(BF16).reshape(far.shape[1:])
@@ -544,7 +576,7 @@
     link.finish()
 
 
-def reduce_out(mixed, w_out, tokens, norm_gains):
+def reduce_out(heads, choice, w_out, tokens, norm_gains):
     width = tokens.shape[1]
     vmem = pl.BlockSpec(memory_space=pltpu.VMEM)
     shape = jax.ShapeDtypeStruct(tokens.shape, BF16)
@@ -553,7 +585,7 @@
     return pl.pallas_call(
         reduce_kernel,
         out_shape=(shape, shape),
-        in_specs=[vmem] * 4,
+        in_specs=[vmem] * 5,
         out_specs=(vmem, vmem),
         scratch_shapes=[
             pltpu.VMEM((2, 4, 2) + piece, BF16),
@@ -573,7 +605,7 @@
         ],
         compiler_params=pltpu.CompilerParams(collective_id=1, has_side_effects=True),
         name="project_reduce",
-    )(mixed, w_out, tokens, norm_gains)
+    )(heads, choice, w_out, tokens, norm_gains)
 
 
 def expert_kernel(
@@ -590,7 +622,7 @@
 
     def fetch(c):
         return pltpu.make_async_copy(
-            w_in.at[pl.ds(c * 512, 512)], raw.at[lax.rem(c, 2)], wsem.at[lax.rem(c, 2)]
+            w_in.at[pl.ds(c * 256, 256)], raw.at[lax.rem(c, 2)], wsem.at[lax.rem(c, 2)]
         )
 
     fetch(0).start()
@@ -629,9 +661,8 @@
 
         fetch(c).wait()
         for b in (0, 1):
-            part = jnp.dot(
-                by2, raw[lax.rem(c, 2), b * 256 : (b + 1) * 256, :], preferred_element_type=F32
-            ).astype(BF16)
+            rows = raw[lax.rem(c, 2), b * 128 : (b + 1) * 128].reshape(256, hidden_units)
+            part = jnp.dot(by2, rows, preferred_element_type=F32).astype(BF16)
             at = pl.ds(pl.multiple_of(c * 256 + b * 128, 128), 128)
             w[at, 0:hidden_units] = part[0:128]
             w[at, hidden_units : 2 * hidden_units] = part[128:256]
@@ -719,7 +750,7 @@
             pltpu.VMEM((16, CAP, width), BF16),
             pltpu.VMEM((16, CAP, width), BF16),
             pltpu.VMEM((16, CAP, width), BF16),
-            pltpu.VMEM((2, 512, units), BF16),
+            pltpu.VMEM((2, 256, 2, units), BF16),
             pltpu.VMEM((width, 2 * units), BF16),
             pltpu.VMEM((units, width), BF16),
             pltpu.VMEM((8 * CAP, 2 * units), F32),
@@ -760,25 +791,25 @@
     width = tokens.shape[1]
     lens = prompt_lens.reshape(-1)
     group = lax.axis_index("req").reshape(1)
-    ids = att_ids.T
-    q, k, v, pages, factors = project(
+    q, k, v, pages, factors, choice = project(
         tokens,
         norm_gains,
         w_query.reshape(width * AEXP, HD),
         w_keyval.reshape(width * 2, HD),
         lens,
-        ids,
+        att_ids.T,
+        att_gates.T,
         page_dest,
         req_adapter,
         page_pool.reshape(page_pool.shape[0], CACHE, 2 * HD),
         adapters.reshape(adapters.shape[0], 4, 8, width),
     )
-    mixed = attend(q, k, v, pages, lens, page_dest, group, ids, att_gates.T)
-    hidden, hnorm = reduce_out(mixed, w_out.reshape(-1, width), tokens, norm_gains)
+    heads = attend(q, k, v, pages, lens, page_dest, group)
+    hidden, hnorm = reduce_out(heads, choice, w_out.reshape(-1, width), tokens, norm_gains)
     return experts(
         hidden,
         hnorm,
-        w_in.reshape(width * 2, -1),
+        w_in,
         w_down,
         moe_ids.T,
         moe_gates.T,

time: 275 us -> 251 us (0.913)
  the two profiles are of different devices: /device:TPU:14 before, /device:TPU:11 now
where the time goes in v3:
time: 251 us; the launch traced here: 248 us
  Pallas kernels  246 us (98%)
    pallas_call x1, Pallas kernels, experts(): pl.pallas_call(expert_kernel, out_shape=jax.ShapeDtypeStruct((rows, width...  100 us
    pallas_call x1, Pallas kernels, project(): pl.pallas_call(project_kernel, out_shape=(jax.ShapeDtypeStruct((rows, 2 *...  62.9 us
    pallas_call x1, Pallas kernels, reduce_out(): pl.pallas_call(reduce_kernel, out_shape=(shape, shape), in_specs=[vmem] *...  49.5 us
    pallas_call x1, Pallas kernels, attend(): pl.pallas_call(attend_kernel, out_shape=jax.ShapeDtypeStruct((rows, 2 * H...  33.4 us

profile of v3, /device:TPU:11, one launch (start us, length us, event | category | flops | bytes accessed | tf_op | source)
XLA Modules:
  0.0 248.0 jit_solution(5003889034256558191)
XLA Ops:
  0.0 62.9 %gather_project.1 = (bf16[2048,256]{1,0:T(8,128)(2,1)}, bf16[2048,128]{1,0:T(8,128)(2,1)}, bf16[2048,128]{1,0:T(8,128)(2,1)}, bf16[8,128,256]{2,1,0:T(8,128)(2,1...) custom-call(s32[4]{0:T(128)} %bitcast.18, s32[32]{0:T(128)} %dest.3, s32[32]{0:T(128)} %wanted.1, bf16[128,2048]{1,0:T(8,128)(2,1)} %tok.3, ...), custom_call_target="tpu_custom_call" | custom-call | tf_op jit(solution)/shard_map/gather_project/pallas_call | solution.py:318
  62.9 33.4 %attend_heads.1.heads = bf16[2048,256]{1,0:T(8,128)(2,1)} custom-call(s32[4]{0:T(128)} %bitcast.19, s32[32]{0:T(128)} %dest.3, s32[1]{0:T(128)} %bitcast.1.group, bf16[2048,256]{1,0:T(8,128)(2,1)} %get-tuple-element.13.q, bf16[2048,128]{1,0:T(8,128)(2,1)} %get-tuple-element.14.k, bf16[2048,128]{1,0:T(8,128)(2,1)} %get-tuple-element.15.v, ...), custom_call_target="tpu_custom_call" | custom-call | tf_op jit(solution)/shard_map/attend_heads/pallas_call | solution.py:436
  96.3 49.5 %project_reduce.1 = (bf16[128,2048]{1,0:T(8,128)(2,1)}, bf16[128,2048]{1,0:T(8,128)(2,1)}) custom-call(bf16[2048,256]{1,0:T(8,128)(2,1)} %attend_heads.1.heads, f32[2048,8]{1,0:T(8,128)} %get-tuple-element.17.choice, bf16[512,2048]{1,0:T(8,128)(2,1)} %bitcast.12, bf16[128,2048]{1,0:T(8,128)(2,1)} %tok.3, f32[2,2048]{1,0:T(2,128)} %gain.3), custom_call_target="tpu_custom_call" | custom-call | tf_op jit(solution)/shard_map/project_reduce/pallas_call | solution.py:585
  145.8 100.3 %expert_exchange.1 = bf16[128,2048]{1,0:T(8,128)(2,1)} custom-call(s32[4]{0:T(128)} %bitcast.20, bf16[128,2048]{1,0:T(8,128)(2,1)} %get-tuple-element.18.hidden, bf16[128,2048]{1,0:T(8,128)(2,1)} %get-tuple-element.19.hnorm, bf16[2048,2,1408]{2,1,0:T(2,128)(2,1)} %w_in.1, bf16[1408,2048]{1,0:T(8,128)(2,1)} %w_down.1, s32[2,128]{1,0:T(2,128)} %bitcast.21, ...), custom_call_target="tpu_custom_call" | custom-call | tf_op jit(solution)/shard_map/expert_exchange/pallas_call | solution.py:743
  246.1 1.9 copy.19
